TPU v7x, 1024 devices: a whole 4x8x16 slice. The times are simulated.
1024 devices in a mesh: pp: 16 (over y_lo, x, core), ep: 64 (over y_hi, z).
Axes of the slice: x: 4, y: 8 (y_hi: 4, y_lo: 2; y = y_hi * 2 + y_lo), z: 16, core: 2. Of those that a mesh axis runs over, the one named last changes fastest.
Arguments:
- x_fwd: bfloat16 [16, 4096, 7168], P('pp', 'ep'), may hold values from -6 to 6
- dy_bwd: bfloat16 [16, 4096, 7168], P('pp', 'ep'), may hold values from -6 to 6
- routes_fwd: int32 [16, 4096, 8], P('pp', 'ep'), may hold values from 0 to 255, as said below
- routes_bwd: int32 [16, 4096, 8], P('pp', 'ep'), may hold values from 0 to 255, as said below
- score_fwd: float32 [16, 4096, 8], P('pp', 'ep'), may hold values from 0.05 to 1
- score_bwd: float32 [16, 4096, 8], P('pp', 'ep'), may hold values from 0.05 to 1
- saved_bwd: float32 [16, 64, 2, 2, 8192], P('pp', None, None, None, 'ep'), may hold values from -6 to 6
- w_gate: bfloat16 [7168, 8192], P(None, 'ep'), may hold values from -0.0625 to 0.0625
- w_up: bfloat16 [7168, 8192], P(None, 'ep'), may hold values from -0.0625 to 0.0625
- w_down: bfloat16 [8192, 7168], P('ep'), may hold values from -0.1875 to 0.1875
Outputs:
- received: bfloat16 [16, 4096, 7168], P('pp', 'ep')
Inputs may be any that keep to these rules, and one draw needn't show every extreme that they name: `routes_fwd`: each token names 8 different ids. Within the 64 tokens of one block of a section, each expert below 8 is named at most 2 times, and in every section some expert below 8 is named exactly 2 times in every block. `routes_bwd`: the same as for routes_fwd.
All inputs are finite; a program needn't handle non-finite values.
Results may differ from a plain program's by a relative error of at most 0.008.
Values may be sent and summed in bfloat16 or wider, within the bound.
No kernel may reach another device: no remote copies, remote signals or barrier semaphores. Data moves between devices by JAX's collectives and lax.ppermute only.
A program may use at most 64 MiB of HBM per device.

v0:
```python
import jax
import jax.numpy as jnp
from jax import lax
from jax.sharding import PartitionSpec as P

SPLIT = 8
CAP = 2


def shifted(value, axis, steps):
    count = lax.axis_size(axis)
    pairs = [(source, (source + steps) % count) for source in range(count)]
    return lax.ppermute(value, axis, pairs)


def route_tables(routes, scores, groups):
    experts = jnp.arange(groups, dtype=jnp.int32)
    match = (routes[:, :, None] == experts).astype(jnp.float32)
    weight = 2.5 * scores / jnp.sum(scores, axis=-1, keepdims=True)
    hits = jnp.sum(match, axis=1)
    shares = jnp.sum(match * weight[:, :, None], axis=1)
    before = jnp.cumsum(hits, axis=0) - hits
    slots = jnp.arange(CAP, dtype=jnp.float32)
    placed = hits[:, :, None] * (before[:, :, None] == slots).astype(jnp.float32)
    return (placed, placed * shares[:, :, None])


def dispatch(values, placed):
    groups = placed.shape[1]
    model_width = values.shape[1]
    buffer = jnp.einsum(
        "tgc,td->gcd", placed.astype(jnp.bfloat16), values, preferred_element_type=jnp.float32
    ).astype(jnp.bfloat16)
    outgoing = jnp.broadcast_to(buffer[:, None], (groups, SPLIT, CAP, model_width))
    outgoing = outgoing.reshape(groups * SPLIT, CAP, model_width)
    return lax.all_to_all(outgoing, "ep", split_axis=0, concat_axis=0, tiled=True)


def forward_partial(token_rows, w_gate, w_up, w_down):
    flat_rows = token_rows.reshape(-1, token_rows.shape[2])
    gate_pre = jnp.dot(flat_rows, w_gate, preferred_element_type=jnp.float32)
    up_pre = jnp.dot(flat_rows, w_up, preferred_element_type=jnp.float32)
    hidden = (jax.nn.silu(gate_pre) * up_pre).astype(jnp.bfloat16)
    partial_value = jnp.dot(hidden, w_down, preferred_element_type=jnp.float32).astype(jnp.bfloat16)
    return partial_value.reshape(token_rows.shape)


def backward_partial(token_rows, saved_rows, w_gate, w_up, w_down):
    contract = (((1,), (1,)), ((), ()))
    flat_rows = token_rows.reshape(-1, token_rows.shape[2])
    gate_saved = saved_rows[:, :, 0].reshape(-1, saved_rows.shape[3])
    up_saved = saved_rows[:, :, 1].reshape(-1, saved_rows.shape[3])
    grad_hidden = lax.dot_general(flat_rows, w_down, contract, preferred_element_type=jnp.float32)
    sigma = jax.nn.sigmoid(gate_saved)
    grad_gate = (grad_hidden * up_saved * sigma * (1.0 + gate_saved * (1.0 - sigma))).astype(
        jnp.bfloat16
    )
    grad_up = (grad_hidden * gate_saved * sigma).astype(jnp.bfloat16)
    partial_value = lax.dot_general(grad_gate, w_gate, contract, preferred_element_type=jnp.float32)
    partial_value = partial_value + lax.dot_general(
        grad_up, w_up, contract, preferred_element_type=jnp.float32
    )
    return partial_value.astype(jnp.bfloat16).reshape(token_rows.shape)


def combine(partial_value, weighted, groups):
    model_width = partial_value.shape[2]
    returned = lax.all_to_all(partial_value, "ep", split_axis=0, concat_axis=0, tiled=True)
    summed = jnp.sum(returned.reshape(groups, SPLIT, CAP, model_width).astype(jnp.float32), axis=1)
    mixed = jnp.einsum("tgc,gcd->td", weighted, summed, precision=lax.Precision.HIGHEST)
    return mixed.astype(jnp.bfloat16)


def body(
    x_fwd, dy_bwd, routes_fwd, routes_bwd, score_fwd, score_bwd, saved_bwd, w_gate, w_up, w_down
):
    groups = lax.axis_size("ep") // SPLIT
    placed_f, weighted_f = route_tables(routes_fwd[0], score_fwd[0], groups)
    rows_f = dispatch(x_fwd[0], placed_f)
    routed_f = combine(forward_partial(rows_f, w_gate, w_up, w_down), weighted_f, groups)
    placed_b, weighted_b = route_tables(routes_bwd[0], score_bwd[0], groups)
    rows_b = dispatch(dy_bwd[0], placed_b)
    routed_b = combine(
        backward_partial(rows_b, saved_bwd[0], w_gate, w_up, w_down), weighted_b, groups
    )
    from_before = shifted(routed_f, "pp", 1)
    from_after = shifted(routed_b, "pp", -1)
    total = from_before.astype(jnp.float32) + from_after.astype(jnp.float32)
    return total.astype(jnp.bfloat16)[None]


def solution(mesh):
    in_specs = (
        P("pp", "ep", None),
        P("pp", "ep", None),
        P("pp", "ep", None),
        P("pp", "ep", None),
        P("pp", "ep", None),
        P("pp", "ep", None),
        P("pp", None, None, None, "ep"),
        P(None, "ep"),
        P(None, "ep"),
        P("ep", None),
    )
    out_specs = P("pp", "ep", None)
    return jax.shard_map(body, mesh=mesh, in_specs=in_specs, out_specs=out_specs, check_vma=False)
```

profile of v0, /device:TPU:1, one launch (start us, length us, event | category | flops | bytes accessed | tf_op | source)
XLA Modules:
  0.0 434.4 jit_solution(4624970621974515921)
XLA Ops:
  0.0 0.8 reduce_sum.77
  0.8 0.7 bitcast_divide_fusion
  1.5 0.7 select_reduce_fusion
  2.5 1.4 convolution_convert_fusion.1
  4.2 2.2 broadcast_in_dim.7
  6.4 25.9 %all-to-all-start.2 = ((bf16[64,2,7168]{2,1,0:T(2,128)(2,1)}), bf16[64,2,7168]{2,1,0:T(2,128)(2,1)}, u32[]{:S(2)}, u32[]{:S(2)}) async-start(bf16[64,2,7168]{2,1,0:T(2,128)(2,1)} %bitcast.44), calls=%async_computation.2 | async-start | bytes 3670016 | tf_op jit(solution)/shard_map/all_to_all | solution.py:36
  32.6 0.2 convolution_convert_fusion.2
  33.1 81.5 %all-to-all-done.2 = bf16[64,2,7168]{2,1,0:T(2,128)(2,1)} async-done(((bf16[64,2,7168]{2,1,0:T(2,128)(2,1)}), bf16[64,2,7168]{2,1,0:T(2,128)(2,1)}, u32[]{:S(2)}, u32[]{:S(2)}) %all-to-all-start.2) | async-done | bytes 1835040 | tf_op jit(solution)/shard_map/all_to_all | solution.py:36
  114.6 2.2 broadcast_in_dim.6
  116.8 14.7 %all-to-all-start = ((bf16[64,2,7168]{2,1,0:T(2,128)(2,1)}), bf16[64,2,7168]{2,1,0:T(2,128)(2,1)}, u32[]{:S(2)}, u32[]{:S(2)}) async-start(bf16[64,2,7168]{2,1,0:T(2,128)(2,1)} %bitcast.45), calls=%async_computation | async-start | bytes 3670016 | tf_op jit(solution)/shard_map/all_to_all | solution.py:36
  131.7 4.9 %reshape.100 = bf16[128,7168]{1,0:T(8,128)(2,1)} reshape(bf16[64,2,7168]{2,1,0:T(2,128)(2,1)} %all-to-all-done.2) | data formatting | bytes 3670016 | tf_op jit(solution)/shard_map/reshape | solution.py:50
  136.7 2.8 fusion.41
  139.5 0.6 fusion.14
  140.2 2.0 fusion
  142.1 4.7 %reshape.101 = bf16[64,2,7168]{2,1,0:T(2,128)(2,1)} reshape(bf16[128,7168]{1,0:T(8,128)(2,1)} %fusion) | data formatting | bytes 3670016 | tf_op jit(solution)/shard_map/reshape | solution.py:63
  146.9 67.4 %all-to-all-done = bf16[64,2,7168]{2,1,0:T(2,128)(2,1)} async-done(((bf16[64,2,7168]{2,1,0:T(2,128)(2,1)}), bf16[64,2,7168]{2,1,0:T(2,128)(2,1)}, u32[]{:S(2)}, u32[]{:S(2)}) %all-to-all-start) | async-done | bytes 1835040 | tf_op jit(solution)/shard_map/all_to_all | solution.py:36
  214.2 14.5 %all-to-all-start.3 = ((bf16[64,2,7168]{2,1,0:T(2,128)(2,1)}), bf16[64,2,7168]{2,1,0:T(2,128)(2,1)}, u32[]{:S(2)}, u32[]{:S(2)}) async-start(bf16[64,2,7168]{2,1,0:T(2,128)(2,1)} %reshape.101), calls=%async_computation.3 | async-start | bytes 3670016 | tf_op jit(solution)/shard_map/all_to_all | solution.py:68
  228.7 4.9 %reshape.97 = bf16[128,7168]{1,0:T(8,128)(2,1)} reshape(bf16[64,2,7168]{2,1,0:T(2,128)(2,1)} %all-to-all-done) | data formatting | bytes 3670016 | tf_op jit(solution)/shard_map/reshape | solution.py:40
  233.7 2.7 fusion.40
  236.3 4.6 %convolution_convert_fusion = bf16[128,7168]{1,0:T(8,128)(2,1)} fusion(bf16[128,7168]{1,0:T(8,128)(2,1)} %param.19, bf16[128,7168]{1,0:T(8,128)(2,1)} %reshape.97, bf16[7168,128]{1,0:T(8,128)(2,1)S(1)} %copy-done, f32[128,128]{1,0:T(8,128)S(1)} %fusion.40), kind=kOutput, calls=%fused_computation.2 | convolution fusion | flops 470777856 | bytes 7405568 | tf_op jit(solution)/shard_map/dot_general | solution.py:44
  240.9 4.8 %reshape.98 = bf16[64,2,7168]{2,1,0:T(2,128)(2,1)} reshape(bf16[128,7168]{1,0:T(8,128)(2,1)} %convolution_convert_fusion) | data formatting | bytes 3670016 | tf_op jit(solution)/shard_map/reshape | solution.py:45
  245.7 65.5 %all-to-all-done.3 = bf16[64,2,7168]{2,1,0:T(2,128)(2,1)} async-done(((bf16[64,2,7168]{2,1,0:T(2,128)(2,1)}), bf16[64,2,7168]{2,1,0:T(2,128)(2,1)}, u32[]{:S(2)}, u32[]{:S(2)}) %all-to-all-start.3) | async-done | bytes 1835040 | tf_op jit(solution)/shard_map/all_to_all | solution.py:68
  311.2 14.3 %all-to-all-start.1 = ((bf16[64,2,7168]{2,1,0:T(2,128)(2,1)}), bf16[64,2,7168]{2,1,0:T(2,128)(2,1)}, u32[]{:S(2)}, u32[]{:S(2)}) async-start(bf16[64,2,7168]{2,1,0:T(2,128)(2,1)} %reshape.98), calls=%async_computation.1 | async-start | bytes 3670016 | tf_op jit(solution)/shard_map/all_to_all | solution.py:68
  325.5 3.3 convert_reduce_fusion
  328.8 1.6 fusion.2
  330.4 2.8 collective-permute-start.1
  333.2 74.9 %all-to-all-done.1 = bf16[64,2,7168]{2,1,0:T(2,128)(2,1)} async-done(((bf16[64,2,7168]{2,1,0:T(2,128)(2,1)}), bf16[64,2,7168]{2,1,0:T(2,128)(2,1)}, u32[]{:S(2)}, u32[]{:S(2)}) %all-to-all-start.1) | async-done | bytes 1835040 | tf_op jit(solution)/shard_map/all_to_all | solution.py:68
  408.1 3.3 convert_reduce_fusion.1
  411.4 1.6 fusion.1
  413.1 8.6 %collective-permute-start = (bf16[64,7168]{1,0:T(8,128)(2,1)S(1)}, bf16[64,7168]{1,0:T(8,128)(2,1)S(1)}, u32[]{:S(2)}, u32[]{:S(2)}) collective-permute-start(bf16[64,7168]{1,0:T(8,128)(2,1)S(1)} %fusion.1), channel_id=1, source_target_pairs={{0,64},{64,128},{128,192},{192,256},{256,320},{320,384},{384,448},... | collective-permute-start | bytes 2752520 | tf_op jit(solution)/shard_map/ppermute | solution.py:13
  421.8 10.3 %collective-permute-done = bf16[64,7168]{1,0:T(8,128)(2,1)S(1)} collective-permute-done((bf16[64,7168]{1,0:T(8,128)(2,1)S(1)}, bf16[64,7168]{1,0:T(8,128)(2,1)S(1)}, u32[]{:S(2)}, u32[]{:S(2)}) %collective-permute-start) | collective-permute-done | bytes 917536 | tf_op jit(solution)/shard_map/ppermute | solution.py:13
  432.1 2.3 fusion.4
  (27 shorter events, 1.1 us)
Async XLA Ops:
  0.0 140.1 %copy-start = (bf16[7168,128]{1,0:T(8,128)(2,1)S(1)}, bf16[7168,128]{1,0:T(8,128)(2,1)}, u32[]{:S(2)}) copy-start(bf16[7168,128]{1,0:T(8,128)(2,1)} %param.18) | copy-start | bytes 5505028
  6.4 25.9 %copy-start.4 = (f32[1,64,8]{1,2,0:T(8,128)S(1)}, f32[1,64,8]{1,2,0:T(8,128)}, u32[]{:S(2)}) copy-start(f32[1,64,8]{1,2,0:T(8,128)} %param.14) | copy-start | bytes 6148
  6.4 26.0 %copy-start.5 = (s32[1,64,8]{1,2,0:T(8,128)S(1)}, s32[1,64,8]{1,2,0:T(8,128)}, u32[]{:S(2)}) copy-start(s32[1,64,8]{1,2,0:T(8,128)} %param.12) | copy-start | bytes 6148
  6.4 26.3 %copy-start.2 = (bf16[1,64,7168]{2,1,0:T(8,128)(2,1)S(1)}, bf16[1,64,7168]{2,1,0:T(8,128)(2,1)}, u32[]{:S(2)}) copy-start(bf16[1,64,7168]{2,1,0:T(8,128)(2,1)} %param.10) | copy-start | bytes 2752516
  6.4 108.3 %all-to-all-start.2 = ((bf16[64,2,7168]{2,1,0:T(2,128)(2,1)}), bf16[64,2,7168]{2,1,0:T(2,128)(2,1)}, u32[]{:S(2)}, u32[]{:S(2)}) async-start(bf16[64,2,7168]{2,1,0:T(2,128)(2,1)} %bitcast.44), calls=%async_computation.2 | async-start | bytes 3670016 | tf_op jit(solution)/shard_map/all_to_all | solution.py:36
  116.8 14.8 %copy-start.3 = (f32[1,64,2,2,128]{4,3,2,1,0:T(2,128)S(1)}, f32[1,64,2,2,128]{4,3,2,1,0:T(2,128)}, u32[]{:S(2)}) copy-start(f32[1,64,2,2,128]{4,3,2,1,0:T(2,128)} %param.16) | copy-start | bytes 393220
  116.8 97.4 %all-to-all-start = ((bf16[64,2,7168]{2,1,0:T(2,128)(2,1)}), bf16[64,2,7168]{2,1,0:T(2,128)(2,1)}, u32[]{:S(2)}, u32[]{:S(2)}) async-start(bf16[64,2,7168]{2,1,0:T(2,128)(2,1)} %bitcast.45), calls=%async_computation | async-start | bytes 3670016 | tf_op jit(solution)/shard_map/all_to_all | solution.py:36
  136.7 2.8 copy-start.1
  214.2 96.9 %all-to-all-start.3 = ((bf16[64,2,7168]{2,1,0:T(2,128)(2,1)}), bf16[64,2,7168]{2,1,0:T(2,128)(2,1)}, u32[]{:S(2)}, u32[]{:S(2)}) async-start(bf16[64,2,7168]{2,1,0:T(2,128)(2,1)} %reshape.101), calls=%async_computation.3 | async-start | bytes 3670016 | tf_op jit(solution)/shard_map/all_to_all | solution.py:68
  311.2 96.9 %all-to-all-start.1 = ((bf16[64,2,7168]{2,1,0:T(2,128)(2,1)}), bf16[64,2,7168]{2,1,0:T(2,128)(2,1)}, u32[]{:S(2)}, u32[]{:S(2)}) async-start(bf16[64,2,7168]{2,1,0:T(2,128)(2,1)} %reshape.98), calls=%async_computation.1 | async-start | bytes 3670016 | tf_op jit(solution)/shard_map/all_to_all | solution.py:68
  330.4 91.3 %collective-permute-start.1 = (bf16[64,7168]{1,0:T(8,128)(2,1)S(1)}, bf16[64,7168]{1,0:T(8,128)(2,1)}, u32[]{:S(2)}, u32[]{:S(2)}) collective-permute-start(bf16[64,7168]{1,0:T(8,128)(2,1)S(1)} %fusion.2), channel_id=1, source_target_pairs={{0,960},{64,0},{128,64},{192,128},{256,192},{320,256},{384,320},{4... | collective-permute-start | bytes 2752520 | tf_op jit(solution)/shard_map/ppermute | solution.py:13
  413.1 19.0 %collective-permute-start = (bf16[64,7168]{1,0:T(8,128)(2,1)S(1)}, bf16[64,7168]{1,0:T(8,128)(2,1)S(1)}, u32[]{:S(2)}, u32[]{:S(2)}) collective-permute-start(bf16[64,7168]{1,0:T(8,128)(2,1)S(1)} %fusion.1), channel_id=1, source_target_pairs={{0,64},{64,128},{128,192},{192,256},{256,320},{320,384},{384,448},... | collective-permute-start | bytes 2752520 | tf_op jit(solution)/shard_map/ppermute | solution.py:13
where the time goes:
time: 437 us; the launch traced here: 434 us
  waiting for transfers between devices  300 us (69%)
  starting transfers between devices  80.9 us (19%)
  local copies, waits for them, and re-layouts  24.7 us (6%)
  matrix products  17.6 us (4%)
  other arithmetic  11.4 us (3%)
    all_to_all x2, waiting for transfers between devices, dispatch(): lax.all_to_all(outgoing, 'ep', split_axis=0, concat_axis=0, tiled=True)  149 us
    all_to_all x2, waiting for transfers between devices, combine(): lax.all_to_all(partial_value, 'ep', split_axis=0, concat_axis=0, tiled=True)  140 us
    all_to_all x2, starting transfers between devices, dispatch(): lax.all_to_all(outgoing, 'ep', split_axis=0, concat_axis=0, tiled=True)  40.7 us
    all_to_all x2, starting transfers between devices, combine(): lax.all_to_all(partial_value, 'ep', split_axis=0, concat_axis=0, tiled=True)  28.8 us
    ppermute x2, starting transfers between devices, shifted(): return lax.ppermute(value, axis, pairs)  11.4 us
    ppermute x2, waiting for transfers between devices, shifted(): return lax.ppermute(value, axis, pairs)  10.3 us
  transfers between devices with their start and end apart: 6, of which 5 were waited for; matrix products, arithmetic and copies ran while one was open for 10% of the time, Pallas kernels for 0%

commit v1 on v0

v1 whole, which is shorter than its diff:
```python
import functools

import jax
import jax.numpy as jnp
import numpy as np
from jax import lax
from jax.experimental import pallas as pl
from jax.experimental.pallas import tpu as pltpu
from jax.sharding import Mesh, PartitionSpec as P

CAP = 2
LANES = 128
HALF = 64
PP = ("ylo", "x", "core")
EP = ("yhi", "zh", "z8")
CHIPS = ("ylo", "x")
Z = ("zh", "z8")
SPREAD = ("ylo", "x", "core", "yhi")
PARTS = (2, 4, 2, 4, 2, 8)
NAMES = PP + EP
INTERPRET = False

BF = jnp.bfloat16
F32 = jnp.float32


def roll_half(value):
    return pltpu.roll(value, HALF, 1)


def low_lanes(shape):
    return lax.broadcasted_iota(jnp.int32, shape, len(shape) - 1) < HALF


def dot_nn(a, b):
    return lax.dot_general(a, b, (((1,), (0,)), ((), ())), preferred_element_type=F32)


def dot_nt(a, b):
    return lax.dot_general(a, b, (((1,), (1,)), ((), ())), preferred_element_type=F32)


def full(shape):
    return pl.BlockSpec(shape, lambda *_: (0,) * len(shape))


def pack_weights_kernel(place, gate, up, down, out):
    core = place[1]
    width = gate.shape[0]
    g = gate[...].astype(F32)
    u = up[...].astype(F32)
    first = jnp.where(core == 0, g, roll_half(g))
    second = jnp.where(core == 0, roll_half(u), u)
    out[:width, :] = jnp.where(low_lanes(g.shape), first, second).astype(BF)
    for i in range(width // LANES):
        out[width + HALF * i : width + HALF * (i + 1), :] = down[:, LANES * i : LANES * (i + 1)]


def pack_weights(place, w_gate, w_up, w_down, width):
    rows = width + HALF * (width // LANES)
    return pl.pallas_call(
        pack_weights_kernel,
        grid_spec=pltpu.PrefetchScalarGridSpec(
            num_scalar_prefetch=1,
            grid=(1,),
            in_specs=[
                pl.BlockSpec((width, LANES), lambda i, s: (s[0], 0)),
                pl.BlockSpec((width, LANES), lambda i, s: (s[0], 0)),
                pl.BlockSpec((HALF, width), lambda i, s: (s[1], s[0])),
            ],
            out_specs=pl.BlockSpec((rows, LANES), lambda i, s: (0, 0)),
        ),
        out_shape=jax.ShapeDtypeStruct((rows, LANES), BF),
        interpret=INTERPRET,
        name="pack_weights",
    )(place, w_gate, w_up, w_down)


def down_pair(weights, width):
    tiles = []
    for i in range(width // LANES):
        lo = width + HALF * i
        tiles.append(jnp.concatenate([weights[0, lo : lo + HALF], weights[1, lo : lo + HALF]], axis=0))
    return jnp.concatenate(tiles, axis=1)


def first_matmul_kernel(rows, weights, out):
    width = rows.shape[3]
    fwd = rows[0, 0]
    bwd = rows[1, 0]
    pair = jnp.concatenate([weights[0, :width], weights[1, :width]], axis=1)
    pre = dot_nn(fwd, pair).astype(BF)
    grad = dot_nt(bwd, down_pair(weights, width)).astype(BF)
    count = out.shape[2]
    for chip in range(out.shape[0]):
        out[chip, 0, :, : 2 * LANES] = pre[chip * count : (chip + 1) * count]
        out[chip, 0, :, 2 * LANES :] = grad[chip * count : (chip + 1) * count]


def first_matmul(rows, weights, chips):
    _, halves, count, width = rows.shape
    pairs = weights.shape[0] // halves // 2
    return pl.pallas_call(
        first_matmul_kernel,
        grid=(halves, pairs),
        in_specs=[
            pl.BlockSpec((2, 1, count, width), lambda h, j: (0, h, 0, 0)),
            pl.BlockSpec((2,) + weights.shape[1:], lambda h, j: (h * pairs + j, 0, 0)),
        ],
        out_specs=pl.BlockSpec((chips, 1, count // chips, 3 * LANES), lambda h, j: (0, h, 0, j)),
        out_shape=jax.ShapeDtypeStruct((chips, halves, count // chips, pairs * 3 * LANES), BF),
        interpret=INTERPRET,
        name="first_matmul",
    )(rows, weights)


def activate_kernel(parts, gates, ups, out):
    chips = parts.shape[0]
    for h in range(parts.shape[1]):
        total = parts[0, h].astype(F32)
        for chip in range(1, chips):
            total = total + parts[chip, h].astype(F32)
        for j in range(parts.shape[3] // (3 * LANES)):
            at = 3 * LANES * j
            hidden = []
            for k in range(2):
                v = total[:, at + LANES * k : at + LANES * (k + 1)]
                hidden.append(v / (1.0 + jnp.exp(-v)) * roll_half(v))
            low = low_lanes(hidden[0].shape)
            hid = jnp.where(low, hidden[0], roll_half(hidden[1]))
            grad = total[:, at + 2 * LANES : at + 3 * LANES]
            gate = gates[h, :, LANES * j : LANES * (j + 1)]
            up = ups[h, :, LANES * j : LANES * (j + 1)]
            sigma = 1.0 / (1.0 + jnp.exp(-gate))
            grad_gate = grad * up * sigma * (1.0 + gate * (1.0 - sigma))
            grad_up = grad * gate * sigma
            tile = jnp.concatenate(
                [
                    jnp.where(low, grad_gate, roll_half(grad_up)),
                    jnp.where(low, roll_half(grad_gate), grad_up),
                    hid,
                ],
                axis=1,
            ).astype(BF)
            for chip in range(chips):
                out[chip, h, :, at : at + 3 * LANES] = tile


def activate(parts, gates, ups):
    return pl.pallas_call(
        activate_kernel,
        out_shape=jax.ShapeDtypeStruct(parts.shape, BF),
        interpret=INTERPRET,
        name="activate",
    )(parts, gates, ups)


def second_matmul_kernel(half, hidden, weights, out, acc):
    width = acc.shape[2]
    chips = hidden.shape[0]
    step = pl.program_id(0)
    rows = jnp.concatenate([hidden[chip, 0] for chip in range(chips)], axis=0)
    fwd = dot_nn(rows[:, 2 * LANES :], down_pair(weights, width))
    pair = jnp.concatenate([weights[0, :width], weights[1, :width]], axis=1)
    bwd = dot_nt(rows[:, : 2 * LANES], pair)

    @pl.when(step == 0)
    def _():
        acc[0] = fwd
        acc[1] = bwd

    @pl.when(step > 0)
    def _():
        acc[0] = acc[0] + fwd
        acc[1] = acc[1] + bwd

    @pl.when(step == pl.num_programs(0) - 1)
    def _():
        out[...] = acc[...].astype(out.dtype)


def second_matmul(half, hidden, weights, width, dtype):
    chips, halves, per_chip, cols = hidden.shape
    pairs = weights.shape[0] // halves // 2
    count = chips * per_chip
    return pl.pallas_call(
        second_matmul_kernel,
        grid_spec=pltpu.PrefetchScalarGridSpec(
            num_scalar_prefetch=1,
            grid=(pairs,),
            in_specs=[
                pl.BlockSpec((chips, 1, per_chip, 3 * LANES), lambda j, s: (0, s[0], 0, j)),
                pl.BlockSpec((2,) + weights.shape[1:], lambda j, s: (s[0] * pairs + j, 0, 0)),
            ],
            out_specs=pl.BlockSpec((2, count, width), lambda j, s: (0, 0, 0)),
            scratch_shapes=[pltpu.VMEM((2, count, width), F32)],
        ),
        out_shape=jax.ShapeDtypeStruct((2, count, width), dtype),
        interpret=INTERPRET,
        name="second_matmul",
    )(half, hidden, weights)


def merge_kernel(kept, other, order, out):
    count = kept.shape[1]
    total = (kept[...] + other[...].astype(F32)).astype(BF)
    out[...] = dot_nn(order[...], total.reshape(2 * count, total.shape[2])).astype(BF)


def merge(kept, other, order):
    _, count, width = kept.shape
    return pl.pallas_call(
        merge_kernel,
        out_shape=jax.ShapeDtypeStruct((2 * count, width), BF),
        interpret=INTERPRET,
        name="merge",
    )(kept, other, order)


def combine_kernel(weight, rows, out):
    w = weight[...]
    top = w.astype(BF)
    rest = w - top.astype(F32)
    mid = rest.astype(BF)
    low = (rest - mid.astype(F32)).astype(BF)
    values = rows[0]
    out[...] = (dot_nn(top, values) + (dot_nn(mid, values) + dot_nn(low, values))).astype(BF)


def combine(weight, rows):
    chips, depth, width = rows.shape
    tokens = weight.shape[0]
    return pl.pallas_call(
        combine_kernel,
        grid=(chips,),
        in_specs=[full(weight.shape), pl.BlockSpec((1, depth, width), lambda q: (q, 0, 0))],
        out_specs=pl.BlockSpec((tokens, width), lambda q: (0, q)),
        out_shape=jax.ShapeDtypeStruct((tokens, chips * width), BF),
        interpret=INTERPRET,
        name="combine",
    )(weight, rows)


def section_order(sections, blocks):
    count = sections * blocks * CAP
    order = np.zeros((sections, blocks, 2, CAP, 2 * count), np.float32)
    for p in range(sections):
        for y in range(blocks):
            for slot in range(CAP):
                for way, source in ((0, (p - 1) % sections), (1, (p + 1) % sections)):
                    order[p, y, way, slot, way * count + (source * blocks + y) * CAP + slot] = 1.0
    return order.reshape(2 * count, 2 * count)


def route_tables(routes, scores, groups):
    experts = jnp.arange(groups, dtype=jnp.int32)
    match = (routes[:, :, None] == experts).astype(F32)
    weight = 2.5 * scores / jnp.sum(scores, axis=-1, keepdims=True)
    hits = jnp.sum(match, axis=1)
    shares = jnp.sum(match * weight[:, :, None], axis=1)
    before = jnp.cumsum(hits, axis=0) - hits
    slots = jnp.arange(CAP, dtype=F32)
    placed = hits[:, :, None] * (before[:, :, None] == slots).astype(F32)
    return (placed, placed * shares[:, :, None])


def gather_rows(values, placed):
    return jnp.einsum(
        "tgc,td->gcd", placed.astype(BF), values, preferred_element_type=F32
    ).astype(BF)


def shifted(value, steps):
    count = lax.axis_size(PP)
    pairs = [(source, (source + steps) % count) for source in range(count)]
    return lax.ppermute(value, PP, pairs)


def all_to_all(value, axes):
    return lax.all_to_all(value, axes, split_axis=0, concat_axis=0, tiled=True)


def body(
    x_fwd, dy_bwd, routes_fwd, routes_bwd, score_fwd, score_bwd, saved_bwd, w_gate, w_up, w_down
):
    chips = lax.axis_size(CHIPS)
    sections = lax.axis_size(PP)
    ny = lax.axis_size("yhi")
    ns = lax.axis_size("z8")
    nz = lax.axis_size(Z)
    groups = 2 * ny
    width = w_gate.shape[0] // chips
    tokens = x_fwd.shape[1]
    core = lax.axis_index("core")
    place = jnp.stack([lax.axis_index(CHIPS), core]).astype(jnp.int32)

    packed = pack_weights(place, w_gate, w_up, w_down, width)
    weights = lax.all_gather(packed, Z, axis=0, tiled=True)
    weights = weights.reshape(nz, packed.shape[0], LANES)

    placed_f, weighted_f = route_tables(routes_fwd[0], score_fwd[0], groups)
    placed_b, weighted_b = route_tables(routes_bwd[0], score_bwd[0], groups)
    rows = jnp.stack([gather_rows(x_fwd[0], placed_f), gather_rows(dy_bwd[0], placed_b)])
    rows = rows.reshape(2, ny, 2, CAP, chips, width).transpose(4, 1, 0, 2, 3, 5)
    rows = jnp.broadcast_to(rows[:, None], (chips, 2) + rows.shape[1:])
    rows = all_to_all(rows.reshape(sections * ny, 4 * CAP, width), SPREAD)
    rows = rows.reshape(sections * ny, 2, 2, CAP, width).transpose(1, 2, 0, 3, 4)
    rows = rows.reshape(2, 2, sections * ny * CAP, width)

    saved = saved_bwd[0].reshape(ny, nz, CAP, 2, 2, HALF).transpose(4, 1, 0, 2, 3, 5)
    saved = all_to_all(saved.reshape(2 * nz, ny * CAP, LANES), ("core",) + Z)
    saved = saved.reshape(2, 2, ns, ny, CAP, 2, HALF).transpose(5, 1, 0, 3, 4, 2, 6)
    saved = saved.reshape(2, 2, 2 * ny * CAP, ns * HALF)

    mix_f = shifted(weighted_f.reshape(tokens, groups * CAP), 1)
    mix_b = shifted(weighted_b.reshape(tokens, groups * CAP), -1)
    mix = jnp.stack([mix_f, mix_b], axis=1).reshape(tokens, 2, ny, 2, CAP).transpose(0, 3, 2, 1, 4)
    mix = mix.reshape(tokens, 4 * ny * CAP)

    parts = all_to_all(first_matmul(rows, weights, chips), CHIPS)
    hidden = all_to_all(activate(parts, saved[0], saved[1]), CHIPS)

    swap = [(0, 1), (1, 0)]
    away = (1 - core).astype(jnp.int32).reshape(1)
    sent = second_matmul(away, hidden, weights, width, BF)
    other = lax.ppermute(sent, "core", swap)
    kept = second_matmul(1 - away, hidden, weights, width, F32)
    order = jnp.asarray(section_order(sections, ny), BF)
    merged = merge(kept, other, order)
    merged = all_to_all(merged.reshape(sections * ny, 2 * CAP, width), SPREAD)
    return combine(mix, merged.reshape(chips, 4 * ny * CAP, width))[None]


def solution(mesh):
    fine = Mesh(mesh.devices.reshape(PARTS), NAMES)
    by_token = P(PP, EP, None)
    in_specs = (by_token,) * 6 + (
        P(PP, None, None, None, EP),
        P(None, EP),
        P(None, EP),
        P(EP, None),
    )
    return jax.shard_map(
        body, mesh=fine, in_specs=in_specs, out_specs=by_token, check_vma=False
    )
```

time: 437 us -> 206 us (0.47)
  waiting for transfers between devices: 300 us -> 81 us
  Pallas kernels: 0 us -> 29.8 us
  starting transfers between devices: 80.9 us -> 63.7 us
  matrix products: 17.6 us -> 0.47 us
  between operations: 0.2 us -> 13.7 us
  local copies, waits for them, and re-layouts: 24.7 us -> 14.4 us
  other arithmetic: 11.4 us -> 1.12 us
    all_to_all x4 -> x5, waiting for transfers between devices: 289 us -> 47.9 us  [all_to_all(): return lax.all_to_all(value, axes, split_axis=0, concat_axis=0, tiled=True)]
    all_gather x0 -> x1, waiting for transfers between devices: none -> 30.1 us  [body(): weights = lax.all_gather(packed, Z, axis=0, tiled=True)]
    pallas_call x0 -> x7, Pallas kernels: none -> 29.8 us  [the longest x2 9.14 us: second_matmul(): pl.pallas_call(second_matmul_kernel, grid_spec=pltpu.PrefetchScalarGridSp...]
    all_to_all x4 -> x5, starting transfers between devices: 69.4 us -> 46.8 us  [all_to_all(): return lax.all_to_all(value, axes, split_axis=0, concat_axis=0, tiled=True)]
    dot_general x9 -> x2, matrix products: 17.6 us -> 0.47 us  [gather_rows(): jnp.einsum('tgc,td->gcd', placed.astype(BF), values, preferred_element_ty...]
    reshape x4 -> x7, local copies, waits for them, and re-layouts: 19.4 us -> 7.04 us  [the longest x1 1.89 us: body(): merged = all_to_all(merged.reshape(sections * ny, 2 * CAP, width), SPREAD)]
    reduce_sum x4 -> x2, other arithmetic: 7.33 us -> 0.03 us  [route_tables(): hits = jnp.sum(match, axis=1)]
    ppermute x2 -> x3, waiting for transfers between devices: 10.3 us -> 3.05 us  [the longest x2 3.04 us: shifted(): return lax.ppermute(value, PP, pairs)]
  transfers between devices with their start and end apart: 6 -> 9, of which waited for: 5 -> 6; matrix products, arithmetic and copies ran while one was open for 10% -> 5% of each run, Pallas kernels for 0% -> 6%
where the time goes in v1:
time: 206 us; the launch traced here: 204 us
  waiting for transfers between devices  81 us (39%)
  starting transfers between devices  63.7 us (31%)
  Pallas kernels  29.8 us (14%)
  local copies, waits for them, and re-layouts  14.4 us (7%)
  between operations  13.7 us (7%)
    all_to_all x5, waiting for transfers between devices, all_to_all(): return lax.all_to_all(value, axes, split_axis=0, concat_axis=0, tiled=True)  47.9 us
    all_to_all x5, starting transfers between devices, all_to_all(): return lax.all_to_all(value, axes, split_axis=0, concat_axis=0, tiled=True)  46.8 us
    all_gather x1, waiting for transfers between devices, body(): weights = lax.all_gather(packed, Z, axis=0, tiled=True)  30.1 us
    ppermute x1, starting transfers between devices, body(): other = lax.ppermute(sent, 'core', swap)  11.4 us
    pallas_call x2, Pallas kernels, second_matmul(): pl.pallas_call(second_matmul_kernel, grid_spec=pltpu.PrefetchScalarGridSp...  9.14 us
    pallas_call x1, Pallas kernels, first_matmul(): pl.pallas_call(first_matmul_kernel, grid=(halves, pairs), in_specs=[pl.Bl...  7.45 us
    pallas_call x1, Pallas kernels, combine(): pl.pallas_call(combine_kernel, grid=(chips,), in_specs=[full(weight.shape...  5.61 us
    ppermute x2, starting transfers between devices, shifted(): return lax.ppermute(value, PP, pairs)  5.55 us
  transfers between devices with their start and end apart: 9, of which 6 were waited for; matrix products, arithmetic and copies ran while one was open for 5% of the time, Pallas kernels for 6%

profile of v1, /device:TPU:1, one launch (start us, length us, event | category | flops | bytes accessed | tf_op | source)
XLA Modules:
  0.0 204.3 jit_solution(9335898380312052345)
XLA Ops:
  7.2 2.9 %pack_weights.1 = bf16[1344,128]{1,0:T(8,128)(2,1)} custom-call(s32[2]{0:T(128)} %pad_add_fusion.place, bf16[7168,128]{1,0:T(8,128)(2,1)} %gate.1, bf16[7168,128]{1,0:T(8,128)(2,1)} %up.1, bf16[128,7168]{1,0:T(8,128)(2,1)} %down.1), custom_call_target="tpu_custom_call" | custom-call | tf_op jit(solution)/shard_map/pack_weights/pallas_call | solution.py:61
  12.6 1.3 reshape.128
  13.9 18.2 %all-to-all-start = ((bf16[64,8,896]{2,1,0:T(8,128)(2,1)}), bf16[64,8,896]{2,1,0:T(8,128)(2,1)S(1)}, u32[]{:S(2)}, u32[]{:S(2)}) async-start(bf16[64,8,896]{2,1,0:T(8,128)(2,1)} %reshape.128), calls=%async_computation | async-start | bytes 1835008 | tf_op jit(solution)/shard_map/all_to_all | solution.py:280
  32.5 0.8 reshape.132
  33.4 25.4 %all-to-all-done = bf16[64,8,896]{2,1,0:T(8,128)(2,1)S(1)} async-done(((bf16[64,8,896]{2,1,0:T(8,128)(2,1)}), bf16[64,8,896]{2,1,0:T(8,128)(2,1)S(1)}, u32[]{:S(2)}, u32[]{:S(2)}) %all-to-all-start) | async-done | bytes 917536 | tf_op jit(solution)/shard_map/all_to_all | solution.py:280
  58.8 12.3 %all-to-all-start.2 = ((f32[32,8,128]{2,1,0:T(8,128)}), f32[32,8,128]{2,1,0:T(8,128)S(1)}, u32[]{:S(2)}, u32[]{:S(2)}) async-start(f32[32,8,128]{2,1,0:T(8,128)} %reshape.132), calls=%async_computation.2 | async-start | bytes 262144 | tf_op jit(solution)/shard_map/all_to_all | solution.py:280
  71.3 0.9 copy.67
  72.3 1.3 reshape.130.rows
  73.5 30.1 %all-gather.2.cloned.1.call-done = bf16[21504,128]{1,0:T(8,128)(2,1)} async-done(((bf16[1344,128]{1,0:T(8,128)(2,1)}), bf16[21504,128]{1,0:T(8,128)(2,1)}) %all-gather.2.cloned.1.call-update) | async-done | bytes 5505040 | tf_op jit(solution)/shard_map/all_gather | solution.py:298
  103.6 7.4 %first_matmul.1 = bf16[8,2,16,1536]{3,2,1,0:T(8,128)(2,1)} custom-call(bf16[2,2,128,896]{3,2,1,0:T(8,128)(2,1)} %reshape.130.rows, bf16[16,1344,128]{2,1,0:T(8,128)(2,1)} %bitcast.55), custom_call_target="tpu_custom_call" | custom-call | tf_op jit(solution)/shard_map/first_matmul/pallas_call | solution.py:103
  111.0 5.1 %all-to-all-start.1 = ((bf16[8,2,16,1536]{3,2,1,0:T(8,128)(2,1)}), bf16[8,2,16,1536]{3,2,1,0:T(8,128)(2,1)S(1)}, u32[]{:S(2)}, u32[]{:S(2)}) async-start(bf16[8,2,16,1536]{3,2,1,0:T(8,128)(2,1)} %first_matmul.1), calls=%async_computation.1 | async-start | bytes 1572864 | tf_op jit(solution)/shard_map/all_to_all | solution.py:280
  116.6 0.7 squeeze.16.gates
  117.4 0.7 squeeze.17.ups
  118.1 6.4 %all-to-all-done.1.parts = bf16[8,2,16,1536]{3,2,1,0:T(8,128)(2,1)S(1)} async-done(((bf16[8,2,16,1536]{3,2,1,0:T(8,128)(2,1)}), bf16[8,2,16,1536]{3,2,1,0:T(8,128)(2,1)S(1)}, u32[]{:S(2)}, u32[]{:S(2)}) %all-to-all-start.1) | async-done | bytes 786464 | tf_op jit(solution)/shard_map/all_to_all | solution.py:280
  124.5 0.9 copy-done.2
  125.4 2.3 %activate.1 = bf16[8,2,16,1536]{3,2,1,0:T(8,128)(2,1)} custom-call(bf16[8,2,16,1536]{3,2,1,0:T(8,128)(2,1)} %copy-done.2, f32[2,16,512]{2,1,0:T(8,128)} %squeeze.16.gates, f32[2,16,512]{2,1,0:T(8,128)} %squeeze.17.ups), custom_call_target="tpu_custom_call" | custom-call | tf_op jit(solution)/shard_map/activate/pallas_call | solution.py:150
  127.7 3.5 %all-to-all-start.3 = ((bf16[8,2,16,1536]{3,2,1,0:T(8,128)(2,1)}), bf16[8,2,16,1536]{3,2,1,0:T(8,128)(2,1)S(1)}, u32[]{:S(2)}, u32[]{:S(2)}) async-start(bf16[8,2,16,1536]{3,2,1,0:T(8,128)(2,1)} %activate.1), calls=%async_computation.3 | async-start | bytes 1572864 | tf_op jit(solution)/shard_map/all_to_all | solution.py:280
  131.3 8.3 %all-to-all-done.3.hidden = bf16[8,2,16,1536]{3,2,1,0:T(8,128)(2,1)S(1)} async-done(((bf16[8,2,16,1536]{3,2,1,0:T(8,128)(2,1)}), bf16[8,2,16,1536]{3,2,1,0:T(8,128)(2,1)S(1)}, u32[]{:S(2)}, u32[]{:S(2)}) %all-to-all-start.3) | async-done | bytes 786464 | tf_op jit(solution)/shard_map/all_to_all | solution.py:280
  139.5 0.9 copy-done.1
  140.4 4.5 %second_matmul.3 = bf16[2,128,896]{2,1,0:T(8,128)(2,1)} custom-call(s32[1]{0:T(128)} %bitcast.14.half, bf16[8,2,16,1536]{3,2,1,0:T(8,128)(2,1)} %copy-done.1, bf16[16,1344,128]{2,1,0:T(8,128)(2,1)} %bitcast.56), custom_call_target="tpu_custom_call" | custom-call | tf_op jit(solution)/shard_map/second_matmul/pallas_call | solution.py:186
  144.9 11.4 %collective-permute-start.2 = (bf16[2,128,896]{2,1,0:T(8,128)(2,1)}, bf16[2,128,896]{2,1,0:T(8,128)(2,1)S(1)}, u32[]{:S(2)}, u32[]{:S(2)}) collective-permute-start(bf16[2,128,896]{2,1,0:T(8,128)(2,1)} %second_matmul.3), channel_id=1, source_target_pairs={{0,64},{64,0},{1,65},{65,1},{2,66},{66,2},{3,67},{67,3},{4,68},{68... | collective-permute-start | bytes 1376264 | tf_op jit(solution)/shard_map/ppermute | solution.py:326
  156.3 4.7 %second_matmul.2.kept = f32[2,128,896]{2,1,0:T(8,128)} custom-call(s32[1]{0:T(128)S(6)} %sub.23.half, bf16[8,2,16,1536]{3,2,1,0:T(8,128)(2,1)} %copy-done.1, bf16[16,1344,128]{2,1,0:T(8,128)(2,1)} %bitcast.57), custom_call_target="tpu_custom_call" | custom-call | tf_op jit(solution)/shard_map/second_matmul/pallas_call | solution.py:186
  160.9 0.8 copy-done.4
  161.7 2.4 %merge.1 = bf16[256,896]{1,0:T(8,128)(2,1)} custom-call(f32[2,128,896]{2,1,0:T(8,128)} %second_matmul.2.kept, bf16[2,128,896]{2,1,0:T(8,128)(2,1)} %copy-done.4, bf16[256,256]{1,0:T(8,128)(2,1)} %constant.36.clone.order), custom_call_target="tpu_custom_call" | custom-call | tf_op jit(solution)/shard_map/merge/pallas_call | solution.py:212
  164.1 1.9 reshape.134
  166.0 7.5 %all-to-all-start.4 = ((bf16[64,4,896]{2,1,0:T(4,128)(2,1)}), bf16[64,4,896]{2,1,0:T(4,128)(2,1)S(1)}, u32[]{:S(2)}, u32[]{:S(2)}) async-start(bf16[64,4,896]{2,1,0:T(4,128)(2,1)} %reshape.134), calls=%async_computation.4 | async-start | bytes 917504 | tf_op jit(solution)/shard_map/all_to_all | solution.py:280
  173.8 2.4 %collective-permute-start.1 = (f32[64,16]{0,1:T(8,128)S(1)}, f32[64,16]{0,1:T(8,128)S(1)}, u32[]{:S(2)}, u32[]{:S(2)}) collective-permute-start(f32[64,16]{0,1:T(8,128)S(1)} %get-tuple-element.12), channel_id=1, source_target_pairs={{0,960},{64,0},{128,64},{192,128},{256,192},{320,256},{384,320},{4... | collective-permute-start | bytes 12296 | tf_op jit(solution)/shard_map/ppermute | solution.py:276
  176.2 3.2 %collective-permute-start = (f32[64,16]{0,1:T(8,128)S(1)}, f32[64,16]{0,1:T(8,128)S(1)}, u32[]{:S(2)}, u32[]{:S(2)}) collective-permute-start(f32[64,16]{0,1:T(8,128)S(1)} %get-tuple-element.11), channel_id=1, source_target_pairs={{0,64},{64,128},{128,192},{192,256},{256,320},{320,384},{384,448},... | collective-permute-start | bytes 12296 | tf_op jit(solution)/shard_map/ppermute | solution.py:276
  179.4 3.0 %collective-permute-done = f32[64,16]{0,1:T(8,128)S(1)} collective-permute-done((f32[64,16]{0,1:T(8,128)S(1)}, f32[64,16]{0,1:T(8,128)S(1)}, u32[]{:S(2)}, u32[]{:S(2)}) %collective-permute-start) | collective-permute-done | bytes 4128 | tf_op jit(solution)/shard_map/ppermute | solution.py:276
  183.2 7.8 %all-to-all-done.4 = bf16[64,4,896]{2,1,0:T(4,128)(2,1)S(1)} async-done(((bf16[64,4,896]{2,1,0:T(4,128)(2,1)}), bf16[64,4,896]{2,1,0:T(4,128)(2,1)S(1)}, u32[]{:S(2)}, u32[]{:S(2)}) %all-to-all-start.4) | async-done | bytes 458784 | tf_op jit(solution)/shard_map/all_to_all | solution.py:280
  190.9 0.9 reshape.135.rows
  191.8 5.6 %combine.1 = bf16[64,7168]{1,0:T(8,128)(2,1)} custom-call(f32[64,32]{1,0:T(8,128)} %copy.71.weight, bf16[8,32,896]{2,1,0:T(8,128)(2,1)} %reshape.135.rows), custom_call_target="tpu_custom_call" | custom-call | tf_op jit(solution)/shard_map/combine/pallas_call | solution.py:233
  (65 shorter events, 4.9 us)
Async XLA Ops:
  6.5 3.9 %copy-start = (bf16[1,64,7168]{2,1,0:T(8,128)(2,1)S(1)}, bf16[1,64,7168]{2,1,0:T(8,128)(2,1)}, u32[]{:S(2)}) copy-start(bf16[1,64,7168]{2,1,0:T(8,128)(2,1)} %param.12) | copy-start | bytes 2752516
  6.5 97.0 %all-gather.2.cloned.1.call-start = ((), (), s32[]{:S(2)}) async-start(), calls=%async_computation.5 | async-start | bytes 5849088 | tf_op jit(solution)/shard_map/all_gather | solution.py:298
  7.2 2.9 %copy-start.6 = (f32[1,64,8]{1,2,0:T(8,128)S(1)}, f32[1,64,8]{1,2,0:T(8,128)}, u32[]{:S(2)}) copy-start(f32[1,64,8]{1,2,0:T(8,128)} %param.16) | copy-start | bytes 6148
  7.2 3.0 %copy-start.8 = (s32[1,64,8]{1,2,0:T(8,128)S(1)}, s32[1,64,8]{1,2,0:T(8,128)}, u32[]{:S(2)}) copy-start(s32[1,64,8]{1,2,0:T(8,128)} %param.14) | copy-start | bytes 6148
  10.1 0.7 copy-start.7
  10.1 0.7 copy-start.9
  10.1 1.2 copy-start.3
  12.6 19.5 %copy-start.5 = (f32[1,64,2,2,128]{4,3,2,1,0:T(2,128)S(1)}, f32[1,64,2,2,128]{4,3,2,1,0:T(2,128)}, u32[]{:S(2)}) copy-start(f32[1,64,2,2,128]{4,3,2,1,0:T(2,128)} %param.17) | copy-start | bytes 393220
  13.9 44.9 %all-to-all-start = ((bf16[64,8,896]{2,1,0:T(8,128)(2,1)}), bf16[64,8,896]{2,1,0:T(8,128)(2,1)S(1)}, u32[]{:S(2)}, u32[]{:S(2)}) async-start(bf16[64,8,896]{2,1,0:T(8,128)(2,1)} %reshape.128), calls=%async_computation | async-start | bytes 1835008 | tf_op jit(solution)/shard_map/all_to_all | solution.py:280
  58.8 52.2 %all-to-all-start.2 = ((f32[32,8,128]{2,1,0:T(8,128)}), f32[32,8,128]{2,1,0:T(8,128)S(1)}, u32[]{:S(2)}, u32[]{:S(2)}) async-start(f32[32,8,128]{2,1,0:T(8,128)} %reshape.132), calls=%async_computation.2 | async-start | bytes 262144 | tf_op jit(solution)/shard_map/all_to_all | solution.py:280
  111.0 13.5 %all-to-all-start.1 = ((bf16[8,2,16,1536]{3,2,1,0:T(8,128)(2,1)}), bf16[8,2,16,1536]{3,2,1,0:T(8,128)(2,1)S(1)}, u32[]{:S(2)}, u32[]{:S(2)}) async-start(bf16[8,2,16,1536]{3,2,1,0:T(8,128)(2,1)} %first_matmul.1), calls=%async_computation.1 | async-start | bytes 1572864 | tf_op jit(solution)/shard_map/all_to_all | solution.py:280
  124.5 0.9 copy-start.2
  127.7 11.8 %all-to-all-start.3 = ((bf16[8,2,16,1536]{3,2,1,0:T(8,128)(2,1)}), bf16[8,2,16,1536]{3,2,1,0:T(8,128)(2,1)S(1)}, u32[]{:S(2)}, u32[]{:S(2)}) async-start(bf16[8,2,16,1536]{3,2,1,0:T(8,128)(2,1)} %activate.1), calls=%async_computation.3 | async-start | bytes 1572864 | tf_op jit(solution)/shard_map/all_to_all | solution.py:280
  139.5 0.9 copy-start.1
  144.9 16.1 %collective-permute-start.2 = (bf16[2,128,896]{2,1,0:T(8,128)(2,1)}, bf16[2,128,896]{2,1,0:T(8,128)(2,1)S(1)}, u32[]{:S(2)}, u32[]{:S(2)}) collective-permute-start(bf16[2,128,896]{2,1,0:T(8,128)(2,1)} %second_matmul.3), channel_id=1, source_target_pairs={{0,64},{64,0},{1,65},{65,1},{2,66},{66,2},{3,67},{67,3},{4,68},{68... | collective-permute-start | bytes 1376264 | tf_op jit(solution)/shard_map/ppermute | solution.py:326
  160.9 0.8 copy-start.4
  166.0 24.9 %all-to-all-start.4 = ((bf16[64,4,896]{2,1,0:T(4,128)(2,1)}), bf16[64,4,896]{2,1,0:T(4,128)(2,1)S(1)}, u32[]{:S(2)}, u32[]{:S(2)}) async-start(bf16[64,4,896]{2,1,0:T(4,128)(2,1)} %reshape.134), calls=%async_computation.4 | async-start | bytes 917504 | tf_op jit(solution)/shard_map/all_to_all | solution.py:280
  173.8 5.6 %collective-permute-start.1 = (f32[64,16]{0,1:T(8,128)S(1)}, f32[64,16]{0,1:T(8,128)S(1)}, u32[]{:S(2)}, u32[]{:S(2)}) collective-permute-start(f32[64,16]{0,1:T(8,128)S(1)} %get-tuple-element.12), channel_id=1, source_target_pairs={{0,960},{64,0},{128,64},{192,128},{256,192},{320,256},{384,320},{4... | collective-permute-start | bytes 12296 | tf_op jit(solution)/shard_map/ppermute | solution.py:276
  176.2 6.3 %collective-permute-start = (f32[64,16]{0,1:T(8,128)S(1)}, f32[64,16]{0,1:T(8,128)S(1)}, u32[]{:S(2)}, u32[]{:S(2)}) collective-permute-start(f32[64,16]{0,1:T(8,128)S(1)} %get-tuple-element.11), channel_id=1, source_target_pairs={{0,64},{64,128},{128,192},{192,256},{256,320},{320,384},{384,448},... | collective-permute-start | bytes 12296 | tf_op jit(solution)/shard_map/ppermute | solution.py:276
Sparse Core Ops, SparseCore 0:
  10.3 93.2 all-gather.1

commit v2 on v1

--- a/solution.py
+++ b/solution.py
@@ -19,6 +19,7 @@
 PARTS = (2, 4, 2, 4, 2, 8)
 NAMES = PP + EP
 INTERPRET = False
+PAIRS = 2
 
 BF = jnp.bfloat16
 F32 = jnp.float32
@@ -45,13 +46,14 @@
 
 
 def pack_weights_kernel(place, gate, up, down, out):
-    core = place[1]
+    first = place[1] == 0
     width = gate.shape[0]
     g = gate[...].astype(F32)
     u = up[...].astype(F32)
-    first = jnp.where(core == 0, g, roll_half(g))
-    second = jnp.where(core == 0, roll_half(u), u)
-    out[:width, :] = jnp.where(low_lanes(g.shape), first, second).astype(BF)
+    low = low_lanes(g.shape)
+    top = jnp.where(low, g, roll_half(u))
+    bottom = jnp.where(low, roll_half(g), u)
+    out[:width, :] = jnp.where(first, top, bottom).astype(BF)
     for i in range(width // LANES):
         out[width + HALF * i : width + HALF * (i + 1), :] = down[:, LANES * i : LANES * (i + 1)]
 
@@ -76,11 +78,13 @@
     )(place, w_gate, w_up, w_down)
 
 
-def down_pair(weights, width):
+def down_pair(weights, at, width):
     tiles = []
     for i in range(width // LANES):
         lo = width + HALF * i
-        tiles.append(jnp.concatenate([weights[0, lo : lo + HALF], weights[1, lo : lo + HALF]], axis=0))
+        tiles.append(
+            jnp.concatenate([weights[at, lo : lo + HALF], weights[at + 1, lo : lo + HALF]], axis=0)
+        )
     return jnp.concatenate(tiles, axis=1)
 
 
@@ -88,26 +92,34 @@
     width = rows.shape[3]
     fwd = rows[0, 0]
     bwd = rows[1, 0]
-    pair = jnp.concatenate([weights[0, :width], weights[1, :width]], axis=1)
-    pre = dot_nn(fwd, pair).astype(BF)
-    grad = dot_nt(bwd, down_pair(weights, width)).astype(BF)
     count = out.shape[2]
-    for chip in range(out.shape[0]):
-        out[chip, 0, :, : 2 * LANES] = pre[chip * count : (chip + 1) * count]
-        out[chip, 0, :, 2 * LANES :] = grad[chip * count : (chip + 1) * count]
+    for j in range(weights.shape[0] // 2):
+        pair = jnp.concatenate([weights[2 * j, :width], weights[2 * j + 1, :width]], axis=1)
+        pre = dot_nn(fwd, pair).astype(BF)
+        grad = dot_nt(bwd, down_pair(weights, 2 * j, width)).astype(BF)
+        at = 3 * LANES * j
+        for chip in range(out.shape[0]):
+            span = slice(chip * count, (chip + 1) * count)
+            out[chip, 0, :, at : at + 2 * LANES] = pre[span]
+            out[chip, 0, :, at + 2 * LANES : at + 3 * LANES] = grad[span]
 
 
 def first_matmul(rows, weights, chips):
     _, halves, count, width = rows.shape
     pairs = weights.shape[0] // halves // 2
+    step = min(PAIRS, pairs)
     return pl.pallas_call(
         first_matmul_kernel,
-        grid=(halves, pairs),
+        grid=(halves, pairs // step),
         in_specs=[
             pl.BlockSpec((2, 1, count, width), lambda h, j: (0, h, 0, 0)),
-            pl.BlockSpec((2,) + weights.shape[1:], lambda h, j: (h * pairs + j, 0, 0)),
+            pl.BlockSpec(
+                (2 * step,) + weights.shape[1:], lambda h, j: (h * (pairs // step) + j, 0, 0)
+            ),
         ],
-        out_specs=pl.BlockSpec((chips, 1, count // chips, 3 * LANES), lambda h, j: (0, h, 0, j)),
+        out_specs=pl.BlockSpec(
+            (chips, 1, count // chips, step * 3 * LANES), lambda h, j: (0, h, 0, j)
+        ),
         out_shape=jax.ShapeDtypeStruct((chips, halves, count // chips, pairs * 3 * LANES), BF),
         interpret=INTERPRET,
         name="first_matmul",
@@ -160,9 +172,13 @@
     chips = hidden.shape[0]
     step = pl.program_id(0)
     rows = jnp.concatenate([hidden[chip, 0] for chip in range(chips)], axis=0)
-    fwd = dot_nn(rows[:, 2 * LANES :], down_pair(weights, width))
-    pair = jnp.concatenate([weights[0, :width], weights[1, :width]], axis=1)
-    bwd = dot_nt(rows[:, : 2 * LANES], pair)
+    pairs = weights.shape[0] // 2
+    hid = [rows[:, 3 * LANES * j + 2 * LANES : 3 * LANES * (j + 1)] for j in range(pairs)]
+    down = [down_pair(weights, 2 * j, width) for j in range(pairs)]
+    fwd = dot_nn(jnp.concatenate(hid, axis=1), jnp.concatenate(down, axis=0))
+    grads = [rows[:, 3 * LANES * j : 3 * LANES * j + 2 * LANES] for j in range(pairs)]
+    both = jnp.concatenate([weights[j, :width] for j in range(2 * pairs)], axis=1)
+    bwd = dot_nt(jnp.concatenate(grads, axis=1), both)
 
     @pl.when(step == 0)
     def _():
@@ -182,15 +198,21 @@
 def second_matmul(half, hidden, weights, width, dtype):
     chips, halves, per_chip, cols = hidden.shape
     pairs = weights.shape[0] // halves // 2
+    step = min(PAIRS, pairs)
     count = chips * per_chip
     return pl.pallas_call(
         second_matmul_kernel,
         grid_spec=pltpu.PrefetchScalarGridSpec(
             num_scalar_prefetch=1,
-            grid=(pairs,),
+            grid=(pairs // step,),
             in_specs=[
-                pl.BlockSpec((chips, 1, per_chip, 3 * LANES), lambda j, s: (0, s[0], 0, j)),
-                pl.BlockSpec((2,) + weights.shape[1:], lambda j, s: (s[0] * pairs + j, 0, 0)),
+                pl.BlockSpec(
+                    (chips, 1, per_chip, step * 3 * LANES), lambda j, s: (0, s[0], 0, j)
+                ),
+                pl.BlockSpec(
+                    (2 * step,) + weights.shape[1:],
+                    lambda j, s: (s[0] * (pairs // step) + j, 0, 0),
+                ),
             ],
             out_specs=pl.BlockSpec((2, count, width), lambda j, s: (0, 0, 0)),
             scratch_shapes=[pltpu.VMEM((2, count, width), F32)],
@@ -204,14 +226,17 @@
 def merge_kernel(kept, other, order, out):
     count = kept.shape[1]
     total = (kept[...] + other[...].astype(F32)).astype(BF)
-    out[...] = dot_nn(order[...], total.reshape(2 * count, total.shape[2])).astype(BF)
+    moved = dot_nn(order[...], total.reshape(2 * count, total.shape[2]))
+    rows = out.shape[1]
+    for i in range(out.shape[0]):
+        out[i] = moved[rows * i : rows * (i + 1)].astype(BF)
 
 
 def merge(kept, other, order):
     _, count, width = kept.shape
     return pl.pallas_call(
         merge_kernel,
-        out_shape=jax.ShapeDtypeStruct((2 * count, width), BF),
+        out_shape=jax.ShapeDtypeStruct((count // CAP, 2 * CAP, width), BF),
         interpret=INTERPRET,
         name="merge",
     )(kept, other, order)
@@ -223,18 +248,24 @@
     rest = w - top.astype(F32)
     mid = rest.astype(BF)
     low = (rest - mid.astype(F32)).astype(BF)
-    values = rows[0]
-    out[...] = (dot_nn(top, values) + (dot_nn(mid, values) + dot_nn(low, values))).astype(BF)
+    stacked = jnp.concatenate([top, mid, low], axis=0)
+    tokens = w.shape[0]
+    width = rows.shape[2]
+    for chip in range(rows.shape[0]):
+        parts = dot_nn(stacked, rows[chip])
+        total = parts[:tokens] + (parts[tokens : 2 * tokens] + parts[2 * tokens :])
+        out[:, width * chip : width * (chip + 1)] = total.astype(BF)
 
 
 def combine(weight, rows):
     chips, depth, width = rows.shape
     tokens = weight.shape[0]
+    step = max(1, chips // 2)
     return pl.pallas_call(
         combine_kernel,
-        grid=(chips,),
-        in_specs=[full(weight.shape), pl.BlockSpec((1, depth, width), lambda q: (q, 0, 0))],
-        out_specs=pl.BlockSpec((tokens, width), lambda q: (0, q)),
+        grid=(chips // step,),
+        in_specs=[full(weight.shape), pl.BlockSpec((step, depth, width), lambda q: (q, 0, 0))],
+        out_specs=pl.BlockSpec((tokens, step * width), lambda q: (0, q)),
         out_shape=jax.ShapeDtypeStruct((tokens, chips * width), BF),
         interpret=INTERPRET,
         name="combine",
@@ -316,18 +347,18 @@
     mix_b = shifted(weighted_b.reshape(tokens, groups * CAP), -1)
     mix = jnp.stack([mix_f, mix_b], axis=1).reshape(tokens, 2, ny, 2, CAP).transpose(0, 3, 2, 1, 4)
     mix = mix.reshape(tokens, 4 * ny * CAP)
+    rows, saved, mix = lax.optimization_barrier((rows, saved, mix))
 
     parts = all_to_all(first_matmul(rows, weights, chips), CHIPS)
     hidden = all_to_all(activate(parts, saved[0], saved[1]), CHIPS)
 
-    swap = [(0, 1), (1, 0)]
     away = (1 - core).astype(jnp.int32).reshape(1)
     sent = second_matmul(away, hidden, weights, width, BF)
-    other = lax.ppermute(sent, "core", swap)
+    other = lax.ppermute(sent, "core", [(0, 1), (1, 0)])
     kept = second_matmul(1 - away, hidden, weights, width, F32)
     order = jnp.asarray(section_order(sections, ny), BF)
     merged = merge(kept, other, order)
-    merged = all_to_all(merged.reshape(sections * ny, 2 * CAP, width), SPREAD)
+    merged = all_to_all(merged, SPREAD)
     return combine(mix, merged.reshape(chips, 4 * ny * CAP, width))[None]
 
 

time: 206 us -> 191 us (0.927)
  Pallas kernels: 29.8 us -> 22.7 us
  waiting for transfers between devices: 81 us -> 76.7 us
  local copies, waits for them, and re-layouts: 14.4 us -> 11.5 us
    all_gather x1, waiting for transfers between devices: 30.1 us -> 10.9 us  [body(): weights = lax.all_gather(packed, Z, axis=0, tiled=True)]
    all_to_all x5, waiting for transfers between devices: 47.9 us -> 62.3 us  [all_to_all(): return lax.all_to_all(value, axes, split_axis=0, concat_axis=0, tiled=True)]
    pallas_call x3, Pallas kernels: 15.5 us -> 10.4 us  [the longest x1 5.27 us: first_matmul(): pl.pallas_call(first_matmul_kernel, grid=(halves, pairs // step), in_spec...]
    reshape x2 -> x1, local copies, waits for them, and re-layouts: 2.59 us -> 0.12 us  [body(): saved = saved.reshape(2, 2, 2 * ny * CAP, ns * HALF)]
  transfers between devices with their start and end apart: 9 -> 9, of which waited for: 6 -> 7; matrix products, arithmetic and copies ran while one was open for 5% -> 5% of each run, Pallas kernels for 6% -> 2%
where the time goes in v2:
time: 191 us; the launch traced here: 190 us
  waiting for transfers between devices  76.7 us (40%)
  starting transfers between devices  64 us (34%)
  Pallas kernels  22.7 us (12%)
  between operations  13.7 us (7%)
  local copies, waits for them, and re-layouts  11.5 us (6%)
    all_to_all x5, waiting for transfers between devices, all_to_all(): return lax.all_to_all(value, axes, split_axis=0, concat_axis=0, tiled=True)  62.3 us
    all_to_all x5, starting transfers between devices, all_to_all(): return lax.all_to_all(value, axes, split_axis=0, concat_axis=0, tiled=True)  46.6 us
    ppermute x1, starting transfers between devices, body(): other = lax.ppermute(sent, 'core', [(0, 1), (1, 0)])  12 us
    all_gather x1, waiting for transfers between devices, body(): weights = lax.all_gather(packed, Z, axis=0, tiled=True)  10.9 us
    pallas_call x2, Pallas kernels, second_matmul(): pl.pallas_call(second_matmul_kernel, grid_spec=pltpu.PrefetchScalarGridSp...  7.09 us
    ppermute x2, starting transfers between devices, shifted(): return lax.ppermute(value, PP, pairs)  5.45 us
    pallas_call x1, Pallas kernels, first_matmul(): pl.pallas_call(first_matmul_kernel, grid=(halves, pairs // step), in_spec...  5.27 us
  transfers between devices with their start and end apart: 9, of which 7 were waited for; matrix products, arithmetic and copies ran while one was open for 5% of the time, Pallas kernels for 2%

profile of v2, /device:TPU:1, one launch (start us, length us, event | category | flops | bytes accessed | tf_op | source)
XLA Modules:
  0.0 190.2 jit_solution(8890495882337596092)
XLA Ops:
  7.2 2.9 %pack_weights.1 = bf16[1344,128]{1,0:T(8,128)(2,1)} custom-call(s32[2]{0:T(128)} %pad_add_fusion.place, bf16[7168,128]{1,0:T(8,128)(2,1)} %gate.1, bf16[7168,128]{1,0:T(8,128)(2,1)} %up.1, bf16[128,7168]{1,0:T(8,128)(2,1)} %down.1), custom_call_target="tpu_custom_call" | custom-call | tf_op jit(solution)/shard_map/pack_weights/pallas_call | solution.py:63
  10.6 0.8 reshape.124
  11.4 20.4 %all-to-all-start.1 = ((f32[32,8,128]{2,1,0:T(8,128)}), f32[32,8,128]{2,1,0:T(8,128)S(1)}, u32[]{:S(2)}, u32[]{:S(2)}) async-start(f32[32,8,128]{2,1,0:T(8,128)} %reshape.124), calls=%async_computation.1 | async-start | bytes 262144 | tf_op jit(solution)/shard_map/all_to_all | solution.py:311
  34.1 1.3 reshape.121
  35.4 12.9 %all-to-all-done.1 = f32[32,8,128]{2,1,0:T(8,128)S(1)} async-done(((f32[32,8,128]{2,1,0:T(8,128)}), f32[32,8,128]{2,1,0:T(8,128)S(1)}, u32[]{:S(2)}, u32[]{:S(2)}) %all-to-all-start.1) | async-done | bytes 131104 | tf_op jit(solution)/shard_map/all_to_all | solution.py:311
  48.3 10.2 %all-to-all-start = ((bf16[64,8,896]{2,1,0:T(8,128)(2,1)}), bf16[64,8,896]{2,1,0:T(8,128)(2,1)S(1)}, u32[]{:S(2)}, u32[]{:S(2)}) async-start(bf16[64,8,896]{2,1,0:T(8,128)(2,1)} %reshape.121), calls=%async_computation | async-start | bytes 1835008 | tf_op jit(solution)/shard_map/all_to_all | solution.py:311
  58.8 3.5 %collective-permute-start = (f32[64,16]{0,1:T(8,128)S(1)}, f32[64,16]{0,1:T(8,128)S(1)}, u32[]{:S(2)}, u32[]{:S(2)}) collective-permute-start(f32[64,16]{0,1:T(8,128)S(1)} %get-tuple-element.17), channel_id=1, source_target_pairs={{0,64},{64,128},{128,192},{192,256},{256,320},{320,384},{384,448},... | collective-permute-start | bytes 12296 | tf_op jit(solution)/shard_map/ppermute | solution.py:307
  62.3 1.9 %collective-permute-start.1 = (f32[64,16]{0,1:T(8,128)S(1)}, f32[64,16]{0,1:T(8,128)S(1)}, u32[]{:S(2)}, u32[]{:S(2)}) collective-permute-start(f32[64,16]{0,1:T(8,128)S(1)} %get-tuple-element.18), channel_id=1, source_target_pairs={{0,960},{64,0},{128,64},{192,128},{256,192},{320,256},{384,320},{4... | collective-permute-start | bytes 12296 | tf_op jit(solution)/shard_map/ppermute | solution.py:307
  64.2 3.4 %collective-permute-done.1 = f32[64,16]{0,1:T(8,128)S(1)} collective-permute-done((f32[64,16]{0,1:T(8,128)S(1)}, f32[64,16]{0,1:T(8,128)S(1)}, u32[]{:S(2)}, u32[]{:S(2)}) %collective-permute-start.1) | collective-permute-done | bytes 4128 | tf_op jit(solution)/shard_map/ppermute | solution.py:307
  68.1 17.0 %all-to-all-done = bf16[64,8,896]{2,1,0:T(8,128)(2,1)S(1)} async-done(((bf16[64,8,896]{2,1,0:T(8,128)(2,1)}), bf16[64,8,896]{2,1,0:T(8,128)(2,1)S(1)}, u32[]{:S(2)}, u32[]{:S(2)}) %all-to-all-start) | async-done | bytes 917536 | tf_op jit(solution)/shard_map/all_to_all | solution.py:311
  85.3 0.9 copy.64
  86.2 1.3 reshape.123.rows
  87.5 10.9 %all-gather.2.cloned.1.call-done = bf16[21504,128]{1,0:T(8,128)(2,1)} async-done(((bf16[1344,128]{1,0:T(8,128)(2,1)}), bf16[21504,128]{1,0:T(8,128)(2,1)}) %all-gather.2.cloned.1.call-update) | async-done | bytes 5505040 | tf_op jit(solution)/shard_map/all_gather | solution.py:329
  98.3 5.3 %first_matmul.1 = bf16[8,2,16,1536]{3,2,1,0:T(8,128)(2,1)} custom-call(bf16[2,2,128,896]{3,2,1,0:T(8,128)(2,1)} %reshape.123.rows, bf16[16,1344,128]{2,1,0:T(8,128)(2,1)} %bitcast.57), custom_call_target="tpu_custom_call" | custom-call | tf_op jit(solution)/shard_map/first_matmul/pallas_call | solution.py:111
  103.6 4.8 %all-to-all-start.2 = ((bf16[8,2,16,1536]{3,2,1,0:T(8,128)(2,1)}), bf16[8,2,16,1536]{3,2,1,0:T(8,128)(2,1)S(1)}, u32[]{:S(2)}, u32[]{:S(2)}) async-start(bf16[8,2,16,1536]{3,2,1,0:T(8,128)(2,1)} %first_matmul.1), calls=%async_computation.2 | async-start | bytes 1572864 | tf_op jit(solution)/shard_map/all_to_all | solution.py:311
  108.4 0.7 slice_bitcast_fusion
  109.1 7.7 %all-to-all-done.2.parts = bf16[8,2,16,1536]{3,2,1,0:T(8,128)(2,1)S(1)} async-done(((bf16[8,2,16,1536]{3,2,1,0:T(8,128)(2,1)}), bf16[8,2,16,1536]{3,2,1,0:T(8,128)(2,1)S(1)}, u32[]{:S(2)}, u32[]{:S(2)}) %all-to-all-start.2) | async-done | bytes 786464 | tf_op jit(solution)/shard_map/all_to_all | solution.py:311
  116.7 0.9 copy-done.2
  117.6 2.3 %activate.1 = bf16[8,2,16,1536]{3,2,1,0:T(8,128)(2,1)} custom-call(bf16[8,2,16,1536]{3,2,1,0:T(8,128)(2,1)} %copy-done.2, f32[2,16,512]{2,1,0:T(8,128)} %get-tuple-element.16.gates, f32[2,16,512]{2,1,0:T(8,128)} %get-tuple-element.15.ups), custom_call_target="tpu_custom_call" | custom-call | tf_op jit(solution)/shard_map/activate/pallas_call | solution.py:162
  119.9 3.5 %all-to-all-start.3 = ((bf16[8,2,16,1536]{3,2,1,0:T(8,128)(2,1)}), bf16[8,2,16,1536]{3,2,1,0:T(8,128)(2,1)S(1)}, u32[]{:S(2)}, u32[]{:S(2)}) async-start(bf16[8,2,16,1536]{3,2,1,0:T(8,128)(2,1)} %activate.1), calls=%async_computation.3 | async-start | bytes 1572864 | tf_op jit(solution)/shard_map/all_to_all | solution.py:311
  123.5 8.3 %all-to-all-done.3.hidden = bf16[8,2,16,1536]{3,2,1,0:T(8,128)(2,1)S(1)} async-done(((bf16[8,2,16,1536]{3,2,1,0:T(8,128)(2,1)}), bf16[8,2,16,1536]{3,2,1,0:T(8,128)(2,1)S(1)}, u32[]{:S(2)}, u32[]{:S(2)}) %all-to-all-start.3) | async-done | bytes 786464 | tf_op jit(solution)/shard_map/all_to_all | solution.py:311
  131.7 0.9 copy-done.1
  132.6 3.5 %second_matmul.3 = bf16[2,128,896]{2,1,0:T(8,128)(2,1)} custom-call(s32[1]{0:T(128)} %bitcast.23.half, bf16[8,2,16,1536]{3,2,1,0:T(8,128)(2,1)} %copy-done.1, bf16[16,1344,128]{2,1,0:T(8,128)(2,1)} %bitcast.58), custom_call_target="tpu_custom_call" | custom-call | tf_op jit(solution)/shard_map/second_matmul/pallas_call | solution.py:203
  136.1 12.0 %collective-permute-start.2 = (bf16[2,128,896]{2,1,0:T(8,128)(2,1)}, bf16[2,128,896]{2,1,0:T(8,128)(2,1)S(1)}, u32[]{:S(2)}, u32[]{:S(2)}) collective-permute-start(bf16[2,128,896]{2,1,0:T(8,128)(2,1)} %second_matmul.3), channel_id=1, source_target_pairs={{0,64},{64,0},{1,65},{65,1},{2,66},{66,2},{3,67},{67,3},{4,68},{68... | collective-permute-start | bytes 1376264 | tf_op jit(solution)/shard_map/ppermute | solution.py:357
  148.1 3.6 %second_matmul.2.kept = f32[2,128,896]{2,1,0:T(8,128)} custom-call(s32[1]{0:T(128)S(6)} %sub.23.half, bf16[8,2,16,1536]{3,2,1,0:T(8,128)(2,1)} %copy-done.1, bf16[16,1344,128]{2,1,0:T(8,128)(2,1)} %bitcast.59), custom_call_target="tpu_custom_call" | custom-call | tf_op jit(solution)/shard_map/second_matmul/pallas_call | solution.py:203
  151.8 0.8 copy-done.4
  152.5 2.4 %merge.1 = bf16[64,4,896]{2,1,0:T(4,128)(2,1)} custom-call(f32[2,128,896]{2,1,0:T(8,128)} %second_matmul.2.kept, bf16[2,128,896]{2,1,0:T(8,128)(2,1)} %copy-done.4, bf16[256,256]{1,0:T(8,128)(2,1)} %constant.36.clone.order), custom_call_target="tpu_custom_call" | custom-call | tf_op jit(solution)/shard_map/merge/pallas_call | solution.py:237
  155.0 7.6 %all-to-all-start.4 = ((bf16[64,4,896]{2,1,0:T(4,128)(2,1)}), bf16[64,4,896]{2,1,0:T(4,128)(2,1)S(1)}, u32[]{:S(2)}, u32[]{:S(2)}) async-start(bf16[64,4,896]{2,1,0:T(4,128)(2,1)} %merge.1), calls=%async_computation.4 | async-start | bytes 917504 | tf_op jit(solution)/shard_map/all_to_all | solution.py:311
  162.6 0.7 copy.68.weight
  163.3 16.5 %all-to-all-done.4 = bf16[64,4,896]{2,1,0:T(4,128)(2,1)S(1)} async-done(((bf16[64,4,896]{2,1,0:T(4,128)(2,1)}), bf16[64,4,896]{2,1,0:T(4,128)(2,1)S(1)}, u32[]{:S(2)}, u32[]{:S(2)}) %all-to-all-start.4) | async-done | bytes 458784 | tf_op jit(solution)/shard_map/all_to_all | solution.py:311
  179.8 0.9 reshape.130.rows
  180.7 2.7 %combine.1 = bf16[64,7168]{1,0:T(8,128)(2,1)} custom-call(f32[64,32]{1,0:T(8,128)} %copy.68.weight, bf16[8,32,896]{2,1,0:T(8,128)(2,1)} %reshape.130.rows), custom_call_target="tpu_custom_call" | custom-call | tf_op jit(solution)/shard_map/combine/pallas_call | solution.py:264
  (62 shorter events, 4.0 us)
Async XLA Ops:
  6.5 26.0 %copy-start = (bf16[1,64,7168]{2,1,0:T(8,128)(2,1)S(1)}, bf16[1,64,7168]{2,1,0:T(8,128)(2,1)}, u32[]{:S(2)}) copy-start(bf16[1,64,7168]{2,1,0:T(8,128)(2,1)} %param.11) | copy-start | bytes 2752516
  6.5 91.8 %all-gather.2.cloned.1.call-start = ((), (), s32[]{:S(2)}) async-start(), calls=%async_computation.5 | async-start | bytes 5849088 | tf_op jit(solution)/shard_map/all_gather | solution.py:329
  7.2 2.9 %copy-start.5 = (f32[1,64,2,2,128]{4,3,2,1,0:T(2,128)S(1)}, f32[1,64,2,2,128]{4,3,2,1,0:T(2,128)}, u32[]{:S(2)}) copy-start(f32[1,64,2,2,128]{4,3,2,1,0:T(2,128)} %param.17) | copy-start | bytes 393220
  10.1 21.7 %copy-start.6 = (f32[1,64,8]{1,2,0:T(8,128)S(1)}, f32[1,64,8]{1,2,0:T(8,128)}, u32[]{:S(2)}) copy-start(f32[1,64,8]{1,2,0:T(8,128)} %param.15) | copy-start | bytes 6148
  10.1 21.8 %copy-start.8 = (s32[1,64,8]{1,2,0:T(8,128)S(1)}, s32[1,64,8]{1,2,0:T(8,128)}, u32[]{:S(2)}) copy-start(s32[1,64,8]{1,2,0:T(8,128)} %param.13) | copy-start | bytes 6148
  10.1 22.0 %copy-start.7 = (f32[1,64,8]{1,2,0:T(8,128)S(1)}, f32[1,64,8]{1,2,0:T(8,128)}, u32[]{:S(2)}) copy-start(f32[1,64,8]{1,2,0:T(8,128)} %param.16) | copy-start | bytes 6148
  10.1 22.1 %copy-start.9 = (s32[1,64,8]{1,2,0:T(8,128)S(1)}, s32[1,64,8]{1,2,0:T(8,128)}, u32[]{:S(2)}) copy-start(s32[1,64,8]{1,2,0:T(8,128)} %param.14) | copy-start | bytes 6148
  10.2 22.6 %copy-start.3 = (bf16[1,64,7168]{2,1,0:T(8,128)(2,1)S(1)}, bf16[1,64,7168]{2,1,0:T(8,128)(2,1)}, u32[]{:S(2)}) copy-start(bf16[1,64,7168]{2,1,0:T(8,128)(2,1)} %param.12) | copy-start | bytes 2752516
  11.4 36.9 %all-to-all-start.1 = ((f32[32,8,128]{2,1,0:T(8,128)}), f32[32,8,128]{2,1,0:T(8,128)S(1)}, u32[]{:S(2)}, u32[]{:S(2)}) async-start(f32[32,8,128]{2,1,0:T(8,128)} %reshape.124), calls=%async_computation.1 | async-start | bytes 262144 | tf_op jit(solution)/shard_map/all_to_all | solution.py:311
  48.3 36.9 %all-to-all-start = ((bf16[64,8,896]{2,1,0:T(8,128)(2,1)}), bf16[64,8,896]{2,1,0:T(8,128)(2,1)S(1)}, u32[]{:S(2)}, u32[]{:S(2)}) async-start(bf16[64,8,896]{2,1,0:T(8,128)(2,1)} %reshape.121), calls=%async_computation | async-start | bytes 1835008 | tf_op jit(solution)/shard_map/all_to_all | solution.py:311
  58.8 5.5 %collective-permute-start = (f32[64,16]{0,1:T(8,128)S(1)}, f32[64,16]{0,1:T(8,128)S(1)}, u32[]{:S(2)}, u32[]{:S(2)}) collective-permute-start(f32[64,16]{0,1:T(8,128)S(1)} %get-tuple-element.17), channel_id=1, source_target_pairs={{0,64},{64,128},{128,192},{192,256},{256,320},{320,384},{384,448},... | collective-permute-start | bytes 12296 | tf_op jit(solution)/shard_map/ppermute | solution.py:307
  62.3 5.4 %collective-permute-start.1 = (f32[64,16]{0,1:T(8,128)S(1)}, f32[64,16]{0,1:T(8,128)S(1)}, u32[]{:S(2)}, u32[]{:S(2)}) collective-permute-start(f32[64,16]{0,1:T(8,128)S(1)} %get-tuple-element.18), channel_id=1, source_target_pairs={{0,960},{64,0},{128,64},{192,128},{256,192},{320,256},{384,320},{4... | collective-permute-start | bytes 12296 | tf_op jit(solution)/shard_map/ppermute | solution.py:307
  103.6 13.1 %all-to-all-start.2 = ((bf16[8,2,16,1536]{3,2,1,0:T(8,128)(2,1)}), bf16[8,2,16,1536]{3,2,1,0:T(8,128)(2,1)S(1)}, u32[]{:S(2)}, u32[]{:S(2)}) async-start(bf16[8,2,16,1536]{3,2,1,0:T(8,128)(2,1)} %first_matmul.1), calls=%async_computation.2 | async-start | bytes 1572864 | tf_op jit(solution)/shard_map/all_to_all | solution.py:311
  116.7 0.9 copy-start.2
  119.9 11.8 %all-to-all-start.3 = ((bf16[8,2,16,1536]{3,2,1,0:T(8,128)(2,1)}), bf16[8,2,16,1536]{3,2,1,0:T(8,128)(2,1)S(1)}, u32[]{:S(2)}, u32[]{:S(2)}) async-start(bf16[8,2,16,1536]{3,2,1,0:T(8,128)(2,1)} %activate.1), calls=%async_computation.3 | async-start | bytes 1572864 | tf_op jit(solution)/shard_map/all_to_all | solution.py:311
  131.7 0.9 copy-start.1
  136.1 15.7 %collective-permute-start.2 = (bf16[2,128,896]{2,1,0:T(8,128)(2,1)}, bf16[2,128,896]{2,1,0:T(8,128)(2,1)S(1)}, u32[]{:S(2)}, u32[]{:S(2)}) collective-permute-start(bf16[2,128,896]{2,1,0:T(8,128)(2,1)} %second_matmul.3), channel_id=1, source_target_pairs={{0,64},{64,0},{1,65},{65,1},{2,66},{66,2},{3,67},{67,3},{4,68},{68... | collective-permute-start | bytes 1376264 | tf_op jit(solution)/shard_map/ppermute | solution.py:357
  151.8 0.8 copy-start.4
  155.0 24.8 %all-to-all-start.4 = ((bf16[64,4,896]{2,1,0:T(4,128)(2,1)}), bf16[64,4,896]{2,1,0:T(4,128)(2,1)S(1)}, u32[]{:S(2)}, u32[]{:S(2)}) async-start(bf16[64,4,896]{2,1,0:T(4,128)(2,1)} %merge.1), calls=%async_computation.4 | async-start | bytes 917504 | tf_op jit(solution)/shard_map/all_to_all | solution.py:311
Sparse Core Ops, SparseCore 0:
  10.3 88.0 all-gather.1

commit v3 on v2

--- a/solution.py
+++ b/solution.py
@@ -41,6 +41,18 @@
     return lax.dot_general(a, b, (((1,), (1,)), ((), ())), preferred_element_type=F32)
 
 
+def in_vmem(value):
+    return value if INTERPRET else pltpu.with_memory_space_constraint(value, pltpu.VMEM)
+
+
+def in_hbm(value):
+    return value if INTERPRET else pltpu.with_memory_space_constraint(value, pltpu.HBM)
+
+
+SMALL = pltpu.CompilerParams(vmem_limit_bytes=20 << 20)
+VMEM_SPEC = pl.BlockSpec(memory_space=pltpu.VMEM)
+
+
 def full(shape):
     return pl.BlockSpec(shape, lambda *_: (0,) * len(shape))
 
@@ -88,42 +100,44 @@
     return jnp.concatenate(tiles, axis=1)
 
 
-def first_matmul_kernel(rows, weights, out):
-    width = rows.shape[3]
-    fwd = rows[0, 0]
-    bwd = rows[1, 0]
-    count = out.shape[2]
-    for j in range(weights.shape[0] // 2):
-        pair = jnp.concatenate([weights[2 * j, :width], weights[2 * j + 1, :width]], axis=1)
-        pre = dot_nn(fwd, pair).astype(BF)
-        grad = dot_nt(bwd, down_pair(weights, 2 * j, width)).astype(BF)
+def first_matmul_kernel(rows, source, out, weights, sems):
+    halves, count, width = rows.shape[1:]
+    chips = out.shape[0]
+    per_chip = count // chips
+    total = weights.shape[0]
+    copies = [
+        pltpu.make_async_copy(source.at[2 * i : 2 * i + 2], weights.at[2 * i : 2 * i + 2], sems.at[i])
+        for i in range(total // 2)
+    ]
+    for copy in copies:
+        copy.start()
+    for i, copy in enumerate(copies):
+        h, j = divmod(i, total // 2 // halves)
+        copy.wait()
+        pair = jnp.concatenate([weights[2 * i, :width], weights[2 * i + 1, :width]], axis=1)
+        pre = dot_nn(rows[0, h], pair).astype(BF)
+        grad = dot_nt(rows[1, h], down_pair(weights, 2 * i, width)).astype(BF)
         at = 3 * LANES * j
-        for chip in range(out.shape[0]):
-            span = slice(chip * count, (chip + 1) * count)
-            out[chip, 0, :, at : at + 2 * LANES] = pre[span]
-            out[chip, 0, :, at + 2 * LANES : at + 3 * LANES] = grad[span]
+        for chip in range(chips):
+            span = slice(chip * per_chip, (chip + 1) * per_chip)
+            out[chip, h, :, at : at + 2 * LANES] = pre[span]
+            out[chip, h, :, at + 2 * LANES : at + 3 * LANES] = grad[span]
 
 
 def first_matmul(rows, weights, chips):
-    _, halves, count, width = rows.shape
-    pairs = weights.shape[0] // halves // 2
-    step = min(PAIRS, pairs)
+    _, halves, count, _ = rows.shape
+    total = weights.shape[0]
+    shape = (chips, halves, count // chips, total // halves // 2 * 3 * LANES)
     return pl.pallas_call(
         first_matmul_kernel,
-        grid=(halves, pairs // step),
-        in_specs=[
-            pl.BlockSpec((2, 1, count, width), lambda h, j: (0, h, 0, 0)),
-            pl.BlockSpec(
-                (2 * step,) + weights.shape[1:], lambda h, j: (h * (pairs // step) + j, 0, 0)
-            ),
-        ],
-        out_specs=pl.BlockSpec(
-            (chips, 1, count // chips, step * 3 * LANES), lambda h, j: (0, h, 0, j)
-        ),
-        out_shape=jax.ShapeDtypeStruct((chips, halves, count // chips, pairs * 3 * LANES), BF),
-        interpret=INTERPRET,
+        in_specs=[VMEM_SPEC, pl.BlockSpec(memory_space=pl.ANY)],
+        out_specs=VMEM_SPEC,
+        out_shape=jax.ShapeDtypeStruct(shape, BF),
+        scratch_shapes=[pltpu.VMEM(weights.shape, BF), pltpu.SemaphoreType.DMA((total // 2,))],
+        interpret=INTERPRET,
+        compiler_params=SMALL,
         name="first_matmul",
-    )(rows, weights)
+    )(in_vmem(rows), in_hbm(weights))
 
 
 def activate_kernel(parts, gates, ups, out):
@@ -141,8 +155,8 @@
             low = low_lanes(hidden[0].shape)
             hid = jnp.where(low, hidden[0], roll_half(hidden[1]))
             grad = total[:, at + 2 * LANES : at + 3 * LANES]
-            gate = gates[h, :, LANES * j : LANES * (j + 1)]
-            up = ups[h, :, LANES * j : LANES * (j + 1)]
+            gate = gates[h, :, LANES * j : LANES * (j + 1)].astype(F32)
+            up = ups[h, :, LANES * j : LANES * (j + 1)].astype(F32)
             sigma = 1.0 / (1.0 + jnp.exp(-gate))
             grad_gate = grad * up * sigma * (1.0 + gate * (1.0 - sigma))
             grad_up = grad * gate * sigma
@@ -161,66 +175,62 @@
 def activate(parts, gates, ups):
     return pl.pallas_call(
         activate_kernel,
+        in_specs=[VMEM_SPEC] * 3,
         out_shape=jax.ShapeDtypeStruct(parts.shape, BF),
         interpret=INTERPRET,
+        compiler_params=SMALL,
         name="activate",
-    )(parts, gates, ups)
-
-
-def second_matmul_kernel(half, hidden, weights, out, acc):
-    width = acc.shape[2]
-    chips = hidden.shape[0]
-    step = pl.program_id(0)
-    rows = jnp.concatenate([hidden[chip, 0] for chip in range(chips)], axis=0)
-    pairs = weights.shape[0] // 2
-    hid = [rows[:, 3 * LANES * j + 2 * LANES : 3 * LANES * (j + 1)] for j in range(pairs)]
-    down = [down_pair(weights, 2 * j, width) for j in range(pairs)]
-    fwd = dot_nn(jnp.concatenate(hid, axis=1), jnp.concatenate(down, axis=0))
-    grads = [rows[:, 3 * LANES * j : 3 * LANES * j + 2 * LANES] for j in range(pairs)]
-    both = jnp.concatenate([weights[j, :width] for j in range(2 * pairs)], axis=1)
-    bwd = dot_nt(jnp.concatenate(grads, axis=1), both)
-
-    @pl.when(step == 0)
-    def _():
-        acc[0] = fwd
-        acc[1] = bwd
-
-    @pl.when(step > 0)
-    def _():
-        acc[0] = acc[0] + fwd
-        acc[1] = acc[1] + bwd
-
-    @pl.when(step == pl.num_programs(0) - 1)
-    def _():
-        out[...] = acc[...].astype(out.dtype)
+    )(in_vmem(parts), in_vmem(gates), in_vmem(ups))
+
+
+def second_matmul_kernel(half, hidden, source, out, weights, sems):
+    h = half[0]
+    width = out.shape[2]
+    slices = weights.shape[0]
+    pairs = slices // 2
+    copies = [
+        pltpu.make_async_copy(
+            source.at[pl.ds(slices * h + 2 * j, 2)], weights.at[2 * j : 2 * j + 2], sems.at[j]
+        )
+        for j in range(pairs)
+    ]
+    for copy in copies:
+        copy.start()
+    rows = jnp.concatenate([hidden[chip, h] for chip in range(hidden.shape[0])], axis=0)
+    fwd = None
+    bwd = None
+    for j, copy in enumerate(copies):
+        copy.wait()
+        at = 3 * LANES * j
+        pair = jnp.concatenate([weights[2 * j, :width], weights[2 * j + 1, :width]], axis=1)
+        more_f = dot_nn(rows[:, at + 2 * LANES : at + 3 * LANES], down_pair(weights, 2 * j, width))
+        more_b = dot_nt(rows[:, at : at + 2 * LANES], pair)
+        fwd = more_f if fwd is None else fwd + more_f
+        bwd = more_b if bwd is None else bwd + more_b
+    out[0] = fwd.astype(out.dtype)
+    out[1] = bwd.astype(out.dtype)
 
 
 def second_matmul(half, hidden, weights, width, dtype):
-    chips, halves, per_chip, cols = hidden.shape
-    pairs = weights.shape[0] // halves // 2
-    step = min(PAIRS, pairs)
-    count = chips * per_chip
+    chips, halves, per_chip, _ = hidden.shape
+    slices = weights.shape[0] // halves
     return pl.pallas_call(
         second_matmul_kernel,
-        grid_spec=pltpu.PrefetchScalarGridSpec(
-            num_scalar_prefetch=1,
-            grid=(pairs // step,),
-            in_specs=[
-                pl.BlockSpec(
-                    (chips, 1, per_chip, step * 3 * LANES), lambda j, s: (0, s[0], 0, j)
-                ),
-                pl.BlockSpec(
-                    (2 * step,) + weights.shape[1:],
-                    lambda j, s: (s[0] * (pairs // step) + j, 0, 0),
-                ),
-            ],
-            out_specs=pl.BlockSpec((2, count, width), lambda j, s: (0, 0, 0)),
-            scratch_shapes=[pltpu.VMEM((2, count, width), F32)],
-        ),
-        out_shape=jax.ShapeDtypeStruct((2, count, width), dtype),
-        interpret=INTERPRET,
+        in_specs=[
+            pl.BlockSpec(memory_space=pltpu.SMEM),
+            VMEM_SPEC,
+            pl.BlockSpec(memory_space=pl.ANY),
+        ],
+        out_specs=VMEM_SPEC,
+        out_shape=jax.ShapeDtypeStruct((2, chips * per_chip, width), dtype),
+        scratch_shapes=[
+            pltpu.VMEM((slices,) + weights.shape[1:], BF),
+            pltpu.SemaphoreType.DMA((slices // 2,)),
+        ],
+        interpret=INTERPRET,
+        compiler_params=SMALL,
         name="second_matmul",
-    )(half, hidden, weights)
+    )(half, in_vmem(hidden), in_hbm(weights))
 
 
 def merge_kernel(kept, other, order, out):
@@ -236,10 +246,12 @@
     _, count, width = kept.shape
     return pl.pallas_call(
         merge_kernel,
+        in_specs=[VMEM_SPEC] * 3,
         out_shape=jax.ShapeDtypeStruct((count // CAP, 2 * CAP, width), BF),
         interpret=INTERPRET,
+        compiler_params=SMALL,
         name="merge",
-    )(kept, other, order)
+    )(in_vmem(kept), in_vmem(other), in_vmem(order))
 
 
 def combine_kernel(weight, rows, out):
@@ -268,8 +280,9 @@
         out_specs=pl.BlockSpec((tokens, step * width), lambda q: (0, q)),
         out_shape=jax.ShapeDtypeStruct((tokens, chips * width), BF),
         interpret=INTERPRET,
+        compiler_params=SMALL,
         name="combine",
-    )(weight, rows)
+    )(weight, in_vmem(rows))
 
 
 def section_order(sections, blocks):
@@ -338,7 +351,7 @@
     rows = rows.reshape(sections * ny, 2, 2, CAP, width).transpose(1, 2, 0, 3, 4)
     rows = rows.reshape(2, 2, sections * ny * CAP, width)
 
-    saved = saved_bwd[0].reshape(ny, nz, CAP, 2, 2, HALF).transpose(4, 1, 0, 2, 3, 5)
+    saved = saved_bwd[0].astype(BF).reshape(ny, nz, CAP, 2, 2, HALF).transpose(4, 1, 0, 2, 3, 5)
     saved = all_to_all(saved.reshape(2 * nz, ny * CAP, LANES), ("core",) + Z)
     saved = saved.reshape(2, 2, ns, ny, CAP, 2, HALF).transpose(5, 1, 0, 3, 4, 2, 6)
     saved = saved.reshape(2, 2, 2 * ny * CAP, ns * HALF)

time: 191 us -> 181 us (0.948)
  Pallas kernels: 22.7 us -> 16.3 us
  local copies, waits for them, and re-layouts: 11.5 us -> 5.53 us
  waiting for transfers between devices: 76.7 us -> 78.7 us
    pallas_call x5, Pallas kernels: 17.1 us -> 11.6 us  [the longest x2 4.87 us: second_matmul(): pl.pallas_call(second_matmul_kernel, in_specs=[pl.BlockSpec(memory_space=...]
    all_gather x1, waiting for transfers between devices: 10.9 us -> 14.1 us  [body(): weights = lax.all_gather(packed, Z, axis=0, tiled=True)]
    unnamed x22 -> x18, local copies, waits for them, and re-layouts: 2.63 us -> 0.09 us
  transfers between devices with their start and end apart: 9 -> 9, of which waited for: 7 -> 7; matrix products, arithmetic and copies ran while one was open for 5% -> 4% of each run, Pallas kernels for 2% -> 1%
where the time goes in v3:
time: 181 us; the launch traced here: 180 us
  waiting for transfers between devices  78.7 us (43%)
  starting transfers between devices  64.5 us (36%)
  Pallas kernels  16.3 us (9%)
  between operations  13.8 us (8%)
  local copies, waits for them, and re-layouts  5.53 us (3%)
    all_to_all x5, waiting for transfers between devices, all_to_all(): return lax.all_to_all(value, axes, split_axis=0, concat_axis=0, tiled=True)  61.1 us
    all_to_all x5, starting transfers between devices, all_to_all(): return lax.all_to_all(value, axes, split_axis=0, concat_axis=0, tiled=True)  46.1 us
    all_gather x1, waiting for transfers between devices, body(): weights = lax.all_gather(packed, Z, axis=0, tiled=True)  14.1 us
    ppermute x1, starting transfers between devices, body(): other = lax.ppermute(sent, 'core', [(0, 1), (1, 0)])  12.9 us
    ppermute x2, starting transfers between devices, shifted(): return lax.ppermute(value, PP, pairs)  5.45 us
    pallas_call x2, Pallas kernels, second_matmul(): pl.pallas_call(second_matmul_kernel, in_specs=[pl.BlockSpec(memory_space=...  4.87 us
    pallas_call x1, Pallas kernels, first_matmul(): pl.pallas_call(first_matmul_kernel, in_specs=[VMEM_SPEC, pl.BlockSpec(mem...  4.52 us
  transfers between devices with their start and end apart: 9, of which 7 were waited for; matrix products, arithmetic and copies ran while one was open for 4% of the time, Pallas kernels for 1%

profile of v3, /device:TPU:1, one launch (start us, length us, event | category | flops | bytes accessed | tf_op | source)
XLA Modules:
  0.0 180.4 jit_solution(11275449563827690212)
XLA Ops:
  6.5 0.6 pad_add_fusion.place
  7.2 2.9 %pack_weights.1 = bf16[1344,128]{1,0:T(8,128)(2,1)} custom-call(s32[2]{0:T(128)} %pad_add_fusion.place, bf16[7168,128]{1,0:T(8,128)(2,1)} %gate.1, bf16[7168,128]{1,0:T(8,128)(2,1)} %up.1, bf16[128,7168]{1,0:T(8,128)(2,1)} %down.1), custom_call_target="tpu_custom_call" | custom-call | tf_op jit(solution)/shard_map/pack_weights/pallas_call | solution.py:75
  10.3 0.7 reshape.127
  11.1 20.4 %all-to-all-start.1 = ((bf16[32,8,128]{2,1,0:T(8,128)(2,1)}), bf16[32,8,128]{2,1,0:T(8,128)(2,1)S(1)}, u32[]{:S(2)}, u32[]{:S(2)}) async-start(bf16[32,8,128]{2,1,0:T(8,128)(2,1)} %reshape.127), calls=%async_computation.1 | async-start | bytes 131072 | tf_op jit(solution)/shard_map/all_to_all | solution.py:324
  32.2 0.2 convolution_convert_fusion.1
  32.5 0.2 convolution_convert_fusion
  32.8 0.5 copy.62
  33.3 0.5 broadcast_in_dim.4
  33.8 1.3 reshape.124
  35.0 10.3 %all-to-all-done.1 = bf16[32,8,128]{2,1,0:T(8,128)(2,1)S(1)} async-done(((bf16[32,8,128]{2,1,0:T(8,128)(2,1)}), bf16[32,8,128]{2,1,0:T(8,128)(2,1)S(1)}, u32[]{:S(2)}, u32[]{:S(2)}) %all-to-all-start.1) | async-done | bytes 65568 | tf_op jit(solution)/shard_map/all_to_all | solution.py:324
  45.3 10.2 %all-to-all-start = ((bf16[64,8,896]{2,1,0:T(8,128)(2,1)}), bf16[64,8,896]{2,1,0:T(8,128)(2,1)S(1)}, u32[]{:S(2)}, u32[]{:S(2)}) async-start(bf16[64,8,896]{2,1,0:T(8,128)(2,1)} %reshape.124), calls=%async_computation | async-start | bytes 1835008 | tf_op jit(solution)/shard_map/all_to_all | solution.py:324
  55.8 3.5 %collective-permute-start = (f32[64,16]{0,1:T(8,128)S(1)}, f32[64,16]{0,1:T(8,128)S(1)}, u32[]{:S(2)}, u32[]{:S(2)}) collective-permute-start(f32[64,16]{0,1:T(8,128)S(1)} %get-tuple-element.17), channel_id=1, source_target_pairs={{0,64},{64,128},{128,192},{192,256},{256,320},{320,384},{384,448},... | collective-permute-start | bytes 12296 | tf_op jit(solution)/shard_map/ppermute | solution.py:320
  59.3 1.9 %collective-permute-start.1 = (f32[64,16]{0,1:T(8,128)S(1)}, f32[64,16]{0,1:T(8,128)S(1)}, u32[]{:S(2)}, u32[]{:S(2)}) collective-permute-start(f32[64,16]{0,1:T(8,128)S(1)} %get-tuple-element.18), channel_id=1, source_target_pairs={{0,960},{64,0},{128,64},{192,128},{256,192},{320,256},{384,320},{4... | collective-permute-start | bytes 12296 | tf_op jit(solution)/shard_map/ppermute | solution.py:320
  61.3 3.4 %collective-permute-done.1 = f32[64,16]{0,1:T(8,128)S(1)} collective-permute-done((f32[64,16]{0,1:T(8,128)S(1)}, f32[64,16]{0,1:T(8,128)S(1)}, u32[]{:S(2)}, u32[]{:S(2)}) %collective-permute-start.1) | collective-permute-done | bytes 4128 | tf_op jit(solution)/shard_map/ppermute | solution.py:320
  64.9 0.1 reshape.129
  65.0 17.1 %all-to-all-done = bf16[64,8,896]{2,1,0:T(8,128)(2,1)S(1)} async-done(((bf16[64,8,896]{2,1,0:T(8,128)(2,1)}), bf16[64,8,896]{2,1,0:T(8,128)(2,1)S(1)}, u32[]{:S(2)}, u32[]{:S(2)}) %all-to-all-start) | async-done | bytes 917536 | tf_op jit(solution)/shard_map/all_to_all | solution.py:324
  82.3 0.9 copy.64
  83.3 0.3 reshape.126.rows
  83.6 14.1 %all-gather.2.cloned.1.call-done = bf16[21504,128]{1,0:T(8,128)(2,1)} async-done(((bf16[1344,128]{1,0:T(8,128)(2,1)}), bf16[21504,128]{1,0:T(8,128)(2,1)}) %all-gather.2.cloned.1.call-update) | async-done | bytes 5505040 | tf_op jit(solution)/shard_map/all_gather | solution.py:342
  97.7 4.5 %first_matmul.1 = bf16[8,2,16,1536]{3,2,1,0:T(8,128)(2,1)} custom-call(bf16[2,2,128,896]{3,2,1,0:T(8,128)(2,1)S(1)} %reshape.126.rows, bf16[16,1344,128]{2,1,0:T(8,128)(2,1)} %bitcast.57), custom_call_target="tpu_custom_call" | custom-call | tf_op jit(solution)/shard_map/first_matmul/pallas_call | solution.py:131
  102.2 5.1 %all-to-all-start.2 = ((bf16[8,2,16,1536]{3,2,1,0:T(8,128)(2,1)}), bf16[8,2,16,1536]{3,2,1,0:T(8,128)(2,1)S(1)}, u32[]{:S(2)}, u32[]{:S(2)}) async-start(bf16[8,2,16,1536]{3,2,1,0:T(8,128)(2,1)} %first_matmul.1), calls=%async_computation.2 | async-start | bytes 1572864 | tf_op jit(solution)/shard_map/all_to_all | solution.py:324
  107.4 8.3 %all-to-all-done.2.parts = bf16[8,2,16,1536]{3,2,1,0:T(8,128)(2,1)S(1)} async-done(((bf16[8,2,16,1536]{3,2,1,0:T(8,128)(2,1)}), bf16[8,2,16,1536]{3,2,1,0:T(8,128)(2,1)S(1)}, u32[]{:S(2)}, u32[]{:S(2)}) %all-to-all-start.2) | async-done | bytes 786464 | tf_op jit(solution)/shard_map/all_to_all | solution.py:324
  115.7 1.1 activate.1
  116.8 3.5 %all-to-all-start.3 = ((bf16[8,2,16,1536]{3,2,1,0:T(8,128)(2,1)}), bf16[8,2,16,1536]{3,2,1,0:T(8,128)(2,1)S(1)}, u32[]{:S(2)}, u32[]{:S(2)}) async-start(bf16[8,2,16,1536]{3,2,1,0:T(8,128)(2,1)} %activate.1), calls=%async_computation.3 | async-start | bytes 1572864 | tf_op jit(solution)/shard_map/all_to_all | solution.py:324
  120.4 8.2 %all-to-all-done.3.hidden = bf16[8,2,16,1536]{3,2,1,0:T(8,128)(2,1)S(1)} async-done(((bf16[8,2,16,1536]{3,2,1,0:T(8,128)(2,1)}), bf16[8,2,16,1536]{3,2,1,0:T(8,128)(2,1)S(1)}, u32[]{:S(2)}, u32[]{:S(2)}) %all-to-all-start.3) | async-done | bytes 786464 | tf_op jit(solution)/shard_map/all_to_all | solution.py:324
  128.6 2.4 %second_matmul.3 = bf16[2,128,896]{2,1,0:T(8,128)(2,1)S(1)} custom-call(s32[1]{0:T(128)} %bitcast.23.half, bf16[8,2,16,1536]{3,2,1,0:T(8,128)(2,1)S(1)} %all-to-all-done.3.hidden, bf16[16,1344,128]{2,1,0:T(8,128)(2,1)} %bitcast.58), custom_call_target="tpu_custom_call" | custom-call | tf_op jit(solution)/shard_map/second_matmul/pallas_call | solution.py:217
  131.0 12.9 %collective-permute-start.2 = (bf16[2,128,896]{2,1,0:T(8,128)(2,1)S(1)}, bf16[2,128,896]{2,1,0:T(8,128)(2,1)S(1)}, u32[]{:S(2)}, u32[]{:S(2)}) collective-permute-start(bf16[2,128,896]{2,1,0:T(8,128)(2,1)S(1)} %second_matmul.3), channel_id=1, source_target_pairs={{0,64},{64,0},{1,65},{65,1},{2,66},{66,2},{3,67},{67,3},{4,68},{68... | collective-permute-start | bytes 1376264 | tf_op jit(solution)/shard_map/ppermute | solution.py:370
  144.0 2.5 %second_matmul.2.kept = f32[2,128,896]{2,1,0:T(8,128)S(1)} custom-call(s32[1]{0:T(128)S(6)} %sub.23.half, bf16[8,2,16,1536]{3,2,1,0:T(8,128)(2,1)S(1)} %all-to-all-done.3.hidden, bf16[16,1344,128]{2,1,0:T(8,128)(2,1)} %bitcast.59), custom_call_target="tpu_custom_call" | custom-call | tf_op jit(solution)/shard_map/second_matmul/pallas_call | solution.py:217
  146.4 1.1 merge.1
  147.6 6.8 %all-to-all-start.4 = ((bf16[64,4,896]{2,1,0:T(4,128)(2,1)}), bf16[64,4,896]{2,1,0:T(4,128)(2,1)S(1)}, u32[]{:S(2)}, u32[]{:S(2)}) async-start(bf16[64,4,896]{2,1,0:T(4,128)(2,1)} %merge.1), calls=%async_computation.4 | async-start | bytes 917504 | tf_op jit(solution)/shard_map/all_to_all | solution.py:324
  154.5 17.1 %all-to-all-done.4 = bf16[64,4,896]{2,1,0:T(4,128)(2,1)S(1)} async-done(((bf16[64,4,896]{2,1,0:T(4,128)(2,1)}), bf16[64,4,896]{2,1,0:T(4,128)(2,1)S(1)}, u32[]{:S(2)}, u32[]{:S(2)}) %all-to-all-start.4) | async-done | bytes 458784 | tf_op jit(solution)/shard_map/all_to_all | solution.py:324
  171.7 1.8 combine.1
  (59 shorter events, 1.7 us)
Async XLA Ops:
  6.5 25.6 %copy-start = (bf16[1,64,7168]{2,1,0:T(8,128)(2,1)S(1)}, bf16[1,64,7168]{2,1,0:T(8,128)(2,1)}, u32[]{:S(2)}) copy-start(bf16[1,64,7168]{2,1,0:T(8,128)(2,1)} %param.11) | copy-start | bytes 2752516
  6.5 91.2 %all-gather.2.cloned.1.call-start = ((), (), s32[]{:S(2)}) async-start(), calls=%async_computation.5 | async-start | bytes 5849088 | tf_op jit(solution)/shard_map/all_gather | solution.py:342
  7.1 2.9 %copy-start.3 = (f32[1,64,2,2,128]{4,3,2,1,0:T(2,128)S(1)}, f32[1,64,2,2,128]{4,3,2,1,0:T(2,128)}, u32[]{:S(2)}) copy-start(f32[1,64,2,2,128]{4,3,2,1,0:T(2,128)} %param.17) | copy-start | bytes 393220
  7.1 24.4 %copy-start.4 = (f32[1,64,8]{1,2,0:T(8,128)S(1)}, f32[1,64,8]{1,2,0:T(8,128)}, u32[]{:S(2)}) copy-start(f32[1,64,8]{1,2,0:T(8,128)} %param.15) | copy-start | bytes 6148
  7.1 24.4 %copy-start.6 = (s32[1,64,8]{1,2,0:T(8,128)S(1)}, s32[1,64,8]{1,2,0:T(8,128)}, u32[]{:S(2)}) copy-start(s32[1,64,8]{1,2,0:T(8,128)} %param.13) | copy-start | bytes 6148
  7.1 24.7 %copy-start.5 = (f32[1,64,8]{1,2,0:T(8,128)S(1)}, f32[1,64,8]{1,2,0:T(8,128)}, u32[]{:S(2)}) copy-start(f32[1,64,8]{1,2,0:T(8,128)} %param.16) | copy-start | bytes 6148
  7.1 24.7 %copy-start.7 = (s32[1,64,8]{1,2,0:T(8,128)S(1)}, s32[1,64,8]{1,2,0:T(8,128)}, u32[]{:S(2)}) copy-start(s32[1,64,8]{1,2,0:T(8,128)} %param.14) | copy-start | bytes 6148
  10.1 22.4 %copy-start.2 = (bf16[1,64,7168]{2,1,0:T(8,128)(2,1)S(1)}, bf16[1,64,7168]{2,1,0:T(8,128)(2,1)}, u32[]{:S(2)}) copy-start(bf16[1,64,7168]{2,1,0:T(8,128)(2,1)} %param.12) | copy-start | bytes 2752516
  11.1 34.2 %all-to-all-start.1 = ((bf16[32,8,128]{2,1,0:T(8,128)(2,1)}), bf16[32,8,128]{2,1,0:T(8,128)(2,1)S(1)}, u32[]{:S(2)}, u32[]{:S(2)}) async-start(bf16[32,8,128]{2,1,0:T(8,128)(2,1)} %reshape.127), calls=%async_computation.1 | async-start | bytes 131072 | tf_op jit(solution)/shard_map/all_to_all | solution.py:324
  45.3 36.8 %all-to-all-start = ((bf16[64,8,896]{2,1,0:T(8,128)(2,1)}), bf16[64,8,896]{2,1,0:T(8,128)(2,1)S(1)}, u32[]{:S(2)}, u32[]{:S(2)}) async-start(bf16[64,8,896]{2,1,0:T(8,128)(2,1)} %reshape.124), calls=%async_computation | async-start | bytes 1835008 | tf_op jit(solution)/shard_map/all_to_all | solution.py:324
  55.8 5.5 %collective-permute-start = (f32[64,16]{0,1:T(8,128)S(1)}, f32[64,16]{0,1:T(8,128)S(1)}, u32[]{:S(2)}, u32[]{:S(2)}) collective-permute-start(f32[64,16]{0,1:T(8,128)S(1)} %get-tuple-element.17), channel_id=1, source_target_pairs={{0,64},{64,128},{128,192},{192,256},{256,320},{320,384},{384,448},... | collective-permute-start | bytes 12296 | tf_op jit(solution)/shard_map/ppermute | solution.py:320
  59.3 5.4 %collective-permute-start.1 = (f32[64,16]{0,1:T(8,128)S(1)}, f32[64,16]{0,1:T(8,128)S(1)}, u32[]{:S(2)}, u32[]{:S(2)}) collective-permute-start(f32[64,16]{0,1:T(8,128)S(1)} %get-tuple-element.18), channel_id=1, source_target_pairs={{0,960},{64,0},{128,64},{192,128},{256,192},{320,256},{384,320},{4... | collective-permute-start | bytes 12296 | tf_op jit(solution)/shard_map/ppermute | solution.py:320
  102.2 13.5 %all-to-all-start.2 = ((bf16[8,2,16,1536]{3,2,1,0:T(8,128)(2,1)}), bf16[8,2,16,1536]{3,2,1,0:T(8,128)(2,1)S(1)}, u32[]{:S(2)}, u32[]{:S(2)}) async-start(bf16[8,2,16,1536]{3,2,1,0:T(8,128)(2,1)} %first_matmul.1), calls=%async_computation.2 | async-start | bytes 1572864 | tf_op jit(solution)/shard_map/all_to_all | solution.py:324
  116.8 11.8 %all-to-all-start.3 = ((bf16[8,2,16,1536]{3,2,1,0:T(8,128)(2,1)}), bf16[8,2,16,1536]{3,2,1,0:T(8,128)(2,1)S(1)}, u32[]{:S(2)}, u32[]{:S(2)}) async-start(bf16[8,2,16,1536]{3,2,1,0:T(8,128)(2,1)} %activate.1), calls=%async_computation.3 | async-start | bytes 1572864 | tf_op jit(solution)/shard_map/all_to_all | solution.py:324
  131.0 15.4 %collective-permute-start.2 = (bf16[2,128,896]{2,1,0:T(8,128)(2,1)S(1)}, bf16[2,128,896]{2,1,0:T(8,128)(2,1)S(1)}, u32[]{:S(2)}, u32[]{:S(2)}) collective-permute-start(bf16[2,128,896]{2,1,0:T(8,128)(2,1)S(1)} %second_matmul.3), channel_id=1, source_target_pairs={{0,64},{64,0},{1,65},{65,1},{2,66},{66,2},{3,67},{67,3},{4,68},{68... | collective-permute-start | bytes 1376264 | tf_op jit(solution)/shard_map/ppermute | solution.py:370
  143.9 2.5 %copy-start.1 = (bf16[256,256]{1,0:T(8,128)(2,1)S(1)}, bf16[256,256]{1,0:T(8,128)(2,1)}, u32[]{:S(2)}) copy-start(bf16[256,256]{1,0:T(8,128)(2,1)} %constant.36.clone.order) | copy-start | bytes 393220
  147.6 24.1 %all-to-all-start.4 = ((bf16[64,4,896]{2,1,0:T(4,128)(2,1)}), bf16[64,4,896]{2,1,0:T(4,128)(2,1)S(1)}, u32[]{:S(2)}, u32[]{:S(2)}) async-start(bf16[64,4,896]{2,1,0:T(4,128)(2,1)} %merge.1), calls=%async_computation.4 | async-start | bytes 917504 | tf_op jit(solution)/shard_map/all_to_all | solution.py:324
Sparse Core Ops, SparseCore 0:
  10.2 87.4 all-gather.1

commit v4 on v3

--- a/solution.py
+++ b/solution.py
@@ -19,7 +19,7 @@
 PARTS = (2, 4, 2, 4, 2, 8)
 NAMES = PP + EP
 INTERPRET = False
-PAIRS = 2
+GROUP = 4
 
 BF = jnp.bfloat16
 F32 = jnp.float32
@@ -57,47 +57,62 @@
     return pl.BlockSpec(shape, lambda *_: (0,) * len(shape))
 
 
-def pack_weights_kernel(place, gate, up, down, out):
-    first = place[1] == 0
-    width = gate.shape[0]
-    g = gate[...].astype(F32)
-    u = up[...].astype(F32)
+def pack_weights_kernel(gate, up, down, out, g_ref, u_ref, d_ref, sems):
+    width = g_ref.shape[0]
+    chip = lax.axis_index("ylo") * lax.axis_size("x") + lax.axis_index("x")
+    core = lax.axis_index("core")
+    rows = pl.ds(pl.multiple_of(chip * width, width), width)
+    half = pl.ds(pl.multiple_of(core * HALF, HALF), HALF)
+    copies = [
+        pltpu.make_async_copy(gate.at[rows], g_ref, sems.at[0]),
+        pltpu.make_async_copy(up.at[rows], u_ref, sems.at[1]),
+        pltpu.make_async_copy(down.at[half, rows], d_ref, sems.at[2]),
+    ]
+    for copy in copies:
+        copy.start()
+    for copy in copies:
+        copy.wait()
+    first = core == 0
+    g = g_ref[...].astype(F32)
+    u = u_ref[...].astype(F32)
     low = low_lanes(g.shape)
     top = jnp.where(low, g, roll_half(u))
     bottom = jnp.where(low, roll_half(g), u)
     out[:width, :] = jnp.where(first, top, bottom).astype(BF)
     for i in range(width // LANES):
-        out[width + HALF * i : width + HALF * (i + 1), :] = down[:, LANES * i : LANES * (i + 1)]
-
-
-def pack_weights(place, w_gate, w_up, w_down, width):
+        out[width + HALF * i : width + HALF * (i + 1), :] = d_ref[:, LANES * i : LANES * (i + 1)]
+
+
+def pack_weights(w_gate, w_up, w_down, width):
     rows = width + HALF * (width // LANES)
     return pl.pallas_call(
         pack_weights_kernel,
-        grid_spec=pltpu.PrefetchScalarGridSpec(
-            num_scalar_prefetch=1,
-            grid=(1,),
-            in_specs=[
-                pl.BlockSpec((width, LANES), lambda i, s: (s[0], 0)),
-                pl.BlockSpec((width, LANES), lambda i, s: (s[0], 0)),
-                pl.BlockSpec((HALF, width), lambda i, s: (s[1], s[0])),
-            ],
-            out_specs=pl.BlockSpec((rows, LANES), lambda i, s: (0, 0)),
-        ),
+        in_specs=[pl.BlockSpec(memory_space=pl.ANY)] * 3,
+        out_specs=VMEM_SPEC,
         out_shape=jax.ShapeDtypeStruct((rows, LANES), BF),
-        interpret=INTERPRET,
+        scratch_shapes=[
+            pltpu.VMEM((width, LANES), BF),
+            pltpu.VMEM((width, LANES), BF),
+            pltpu.VMEM((HALF, width), BF),
+            pltpu.SemaphoreType.DMA((3,)),
+        ],
+        interpret=INTERPRET,
+        compiler_params=SMALL,
         name="pack_weights",
-    )(place, w_gate, w_up, w_down)
-
-
-def down_pair(weights, at, width):
+    )(in_hbm(w_gate), in_hbm(w_up), in_hbm(w_down))
+
+
+def down_rows(weights, at, count, width):
     tiles = []
     for i in range(width // LANES):
         lo = width + HALF * i
-        tiles.append(
-            jnp.concatenate([weights[at, lo : lo + HALF], weights[at + 1, lo : lo + HALF]], axis=0)
-        )
+        parts = [weights[at + k, lo : lo + HALF] for k in range(count)]
+        tiles.append(jnp.concatenate(parts, axis=0))
     return jnp.concatenate(tiles, axis=1)
+
+
+def up_columns(weights, at, count, width):
+    return jnp.concatenate([weights[at + k, :width] for k in range(count)], axis=1)
 
 
 def first_matmul_kernel(rows, source, out, weights, sems):
@@ -106,22 +121,26 @@
     per_chip = count // chips
     total = weights.shape[0]
     copies = [
-        pltpu.make_async_copy(source.at[2 * i : 2 * i + 2], weights.at[2 * i : 2 * i + 2], sems.at[i])
-        for i in range(total // 2)
+        pltpu.make_async_copy(
+            source.at[GROUP * i : GROUP * (i + 1)], weights.at[GROUP * i : GROUP * (i + 1)], sems.at[i]
+        )
+        for i in range(total // GROUP)
     ]
     for copy in copies:
         copy.start()
     for i, copy in enumerate(copies):
-        h, j = divmod(i, total // 2 // halves)
+        h, j = divmod(i, total // GROUP // halves)
         copy.wait()
-        pair = jnp.concatenate([weights[2 * i, :width], weights[2 * i + 1, :width]], axis=1)
-        pre = dot_nn(rows[0, h], pair).astype(BF)
-        grad = dot_nt(rows[1, h], down_pair(weights, 2 * i, width)).astype(BF)
-        at = 3 * LANES * j
+        pre = dot_nn(rows[0, h], up_columns(weights, GROUP * i, GROUP, width)).astype(BF)
+        grad = dot_nt(rows[1, h], down_rows(weights, GROUP * i, GROUP, width)).astype(BF)
         for chip in range(chips):
             span = slice(chip * per_chip, (chip + 1) * per_chip)
-            out[chip, h, :, at : at + 2 * LANES] = pre[span]
-            out[chip, h, :, at + 2 * LANES : at + 3 * LANES] = grad[span]
+            for k in range(GROUP // 2):
+                at = 3 * LANES * (j * GROUP // 2 + k)
+                out[chip, h, :, at : at + 2 * LANES] = pre[span, 2 * LANES * k : 2 * LANES * (k + 1)]
+                out[chip, h, :, at + 2 * LANES : at + 3 * LANES] = grad[
+                    span, LANES * k : LANES * (k + 1)
+                ]
 
 
 def first_matmul(rows, weights, chips):
@@ -133,7 +152,7 @@
         in_specs=[VMEM_SPEC, pl.BlockSpec(memory_space=pl.ANY)],
         out_specs=VMEM_SPEC,
         out_shape=jax.ShapeDtypeStruct(shape, BF),
-        scratch_shapes=[pltpu.VMEM(weights.shape, BF), pltpu.SemaphoreType.DMA((total // 2,))],
+        scratch_shapes=[pltpu.VMEM(weights.shape, BF), pltpu.SemaphoreType.DMA((total // GROUP,))],
         interpret=INTERPRET,
         compiler_params=SMALL,
         name="first_matmul",
@@ -187,12 +206,13 @@
     h = half[0]
     width = out.shape[2]
     slices = weights.shape[0]
-    pairs = slices // 2
     copies = [
         pltpu.make_async_copy(
-            source.at[pl.ds(slices * h + 2 * j, 2)], weights.at[2 * j : 2 * j + 2], sems.at[j]
+            source.at[pl.ds(slices * h + GROUP * j, GROUP)],
+            weights.at[GROUP * j : GROUP * (j + 1)],
+            sems.at[j],
         )
-        for j in range(pairs)
+        for j in range(slices // GROUP)
     ]
     for copy in copies:
         copy.start()
@@ -201,10 +221,11 @@
     bwd = None
     for j, copy in enumerate(copies):
         copy.wait()
-        at = 3 * LANES * j
-        pair = jnp.concatenate([weights[2 * j, :width], weights[2 * j + 1, :width]], axis=1)
-        more_f = dot_nn(rows[:, at + 2 * LANES : at + 3 * LANES], down_pair(weights, 2 * j, width))
-        more_b = dot_nt(rows[:, at : at + 2 * LANES], pair)
+        ats = [3 * LANES * (j * GROUP // 2 + k) for k in range(GROUP // 2)]
+        hid = jnp.concatenate([rows[:, at + 2 * LANES : at + 3 * LANES] for at in ats], axis=1)
+        grads = jnp.concatenate([rows[:, at : at + 2 * LANES] for at in ats], axis=1)
+        more_f = dot_nn(hid, down_rows(weights, GROUP * j, GROUP, width))
+        more_b = dot_nt(grads, up_columns(weights, GROUP * j, GROUP, width))
         fwd = more_f if fwd is None else fwd + more_f
         bwd = more_b if bwd is None else bwd + more_b
     out[0] = fwd.astype(out.dtype)
@@ -225,7 +246,7 @@
         out_shape=jax.ShapeDtypeStruct((2, chips * per_chip, width), dtype),
         scratch_shapes=[
             pltpu.VMEM((slices,) + weights.shape[1:], BF),
-            pltpu.SemaphoreType.DMA((slices // 2,)),
+            pltpu.SemaphoreType.DMA((slices // GROUP,)),
         ],
         interpret=INTERPRET,
         compiler_params=SMALL,
@@ -336,9 +357,8 @@
     width = w_gate.shape[0] // chips
     tokens = x_fwd.shape[1]
     core = lax.axis_index("core")
-    place = jnp.stack([lax.axis_index(CHIPS), core]).astype(jnp.int32)
-
-    packed = pack_weights(place, w_gate, w_up, w_down, width)
+
+    packed = pack_weights(w_gate, w_up, w_down, width)
     weights = lax.all_gather(packed, Z, axis=0, tiled=True)
     weights = weights.reshape(nz, packed.shape[0], LANES)
 

time: 181 us -> 181 us (level)
  no operation moved by 1% of the time
where the time goes in v4:
time: 181 us; the launch traced here: 180 us
  waiting for transfers between devices  79.9 us (44%)
  starting transfers between devices  64.4 us (36%)
  Pallas kernels  15.6 us (9%)
  between operations  13.8 us (8%)
  local copies, waits for them, and re-layouts  5.53 us (3%)
    all_to_all x5, waiting for transfers between devices, all_to_all(): return lax.all_to_all(value, axes, split_axis=0, concat_axis=0, tiled=True)  61.1 us
    all_to_all x5, starting transfers between devices, all_to_all(): return lax.all_to_all(value, axes, split_axis=0, concat_axis=0, tiled=True)  46.3 us
    all_gather x1, waiting for transfers between devices, body(): weights = lax.all_gather(packed, Z, axis=0, tiled=True)  15.3 us
    ppermute x1, starting transfers between devices, body(): other = lax.ppermute(sent, 'core', [(0, 1), (1, 0)])  12.6 us
    ppermute x2, starting transfers between devices, shifted(): return lax.ppermute(value, PP, pairs)  5.45 us
    pallas_call x2, Pallas kernels, second_matmul(): pl.pallas_call(second_matmul_kernel, in_specs=[pl.BlockSpec(memory_space=...  5.34 us
    pallas_call x1, Pallas kernels, first_matmul(): pl.pallas_call(first_matmul_kernel, in_specs=[VMEM_SPEC, pl.BlockSpec(mem...  4.04 us
  transfers between devices with their start and end apart: 9, of which 7 were waited for; matrix products, arithmetic and copies ran while one was open for 4% of the time, Pallas kernels for 1%

profile of v4, /device:TPU:1, one launch (start us, length us, event | category | flops | bytes accessed | tf_op | source)
XLA Modules:
  0.0 180.2 jit_solution(13681581468574923508)
XLA Ops:
  6.6 2.2 %pack_weights.1 = bf16[1344,128]{1,0:T(8,128)(2,1)} custom-call(bf16[7168,128]{1,0:T(8,128)(2,1)} %gate.1, bf16[7168,128]{1,0:T(8,128)(2,1)} %up.1, bf16[128,7168]{1,0:T(8,128)(2,1)} %down.1), custom_call_target="tpu_custom_call" | custom-call | tf_op jit(solution)/shard_map/pack_weights/pallas_call | solution.py:88
  9.1 0.7 reshape.127
  9.8 20.4 %all-to-all-start.1 = ((bf16[32,8,128]{2,1,0:T(8,128)(2,1)}), bf16[32,8,128]{2,1,0:T(8,128)(2,1)S(1)}, u32[]{:S(2)}, u32[]{:S(2)}) async-start(bf16[32,8,128]{2,1,0:T(8,128)(2,1)} %reshape.127), calls=%async_computation.1 | async-start | bytes 131072 | tf_op jit(solution)/shard_map/all_to_all | solution.py:345
  30.9 0.2 convolution_convert_fusion.1
  31.2 0.2 convolution_convert_fusion
  31.6 0.5 copy.62
  32.1 0.5 broadcast_in_dim.4
  32.5 1.3 reshape.124
  33.8 10.3 %all-to-all-done.1 = bf16[32,8,128]{2,1,0:T(8,128)(2,1)S(1)} async-done(((bf16[32,8,128]{2,1,0:T(8,128)(2,1)}), bf16[32,8,128]{2,1,0:T(8,128)(2,1)S(1)}, u32[]{:S(2)}, u32[]{:S(2)}) %all-to-all-start.1) | async-done | bytes 65568 | tf_op jit(solution)/shard_map/all_to_all | solution.py:345
  44.1 10.2 %all-to-all-start = ((bf16[64,8,896]{2,1,0:T(8,128)(2,1)}), bf16[64,8,896]{2,1,0:T(8,128)(2,1)S(1)}, u32[]{:S(2)}, u32[]{:S(2)}) async-start(bf16[64,8,896]{2,1,0:T(8,128)(2,1)} %reshape.124), calls=%async_computation | async-start | bytes 1835008 | tf_op jit(solution)/shard_map/all_to_all | solution.py:345
  54.6 3.5 %collective-permute-start = (f32[64,16]{0,1:T(8,128)S(1)}, f32[64,16]{0,1:T(8,128)S(1)}, u32[]{:S(2)}, u32[]{:S(2)}) collective-permute-start(f32[64,16]{0,1:T(8,128)S(1)} %get-tuple-element.17), channel_id=1, source_target_pairs={{0,64},{64,128},{128,192},{192,256},{256,320},{320,384},{384,448},... | collective-permute-start | bytes 12296 | tf_op jit(solution)/shard_map/ppermute | solution.py:341
  58.1 1.9 %collective-permute-start.1 = (f32[64,16]{0,1:T(8,128)S(1)}, f32[64,16]{0,1:T(8,128)S(1)}, u32[]{:S(2)}, u32[]{:S(2)}) collective-permute-start(f32[64,16]{0,1:T(8,128)S(1)} %get-tuple-element.18), channel_id=1, source_target_pairs={{0,960},{64,0},{128,64},{192,128},{256,192},{320,256},{384,320},{4... | collective-permute-start | bytes 12296 | tf_op jit(solution)/shard_map/ppermute | solution.py:341
  60.0 3.4 %collective-permute-done.1 = f32[64,16]{0,1:T(8,128)S(1)} collective-permute-done((f32[64,16]{0,1:T(8,128)S(1)}, f32[64,16]{0,1:T(8,128)S(1)}, u32[]{:S(2)}, u32[]{:S(2)}) %collective-permute-start.1) | collective-permute-done | bytes 4128 | tf_op jit(solution)/shard_map/ppermute | solution.py:341
  63.7 0.1 reshape.129
  63.8 17.1 %all-to-all-done = bf16[64,8,896]{2,1,0:T(8,128)(2,1)S(1)} async-done(((bf16[64,8,896]{2,1,0:T(8,128)(2,1)}), bf16[64,8,896]{2,1,0:T(8,128)(2,1)S(1)}, u32[]{:S(2)}, u32[]{:S(2)}) %all-to-all-start) | async-done | bytes 917536 | tf_op jit(solution)/shard_map/all_to_all | solution.py:345
  80.9 0.1 copy.63
  81.1 0.9 copy.64
  82.0 0.3 reshape.126.rows
  82.4 15.3 %all-gather.2.cloned.1.call-done = bf16[21504,128]{1,0:T(8,128)(2,1)} async-done(((bf16[1344,128]{1,0:T(8,128)(2,1)}), bf16[21504,128]{1,0:T(8,128)(2,1)}) %all-gather.2.cloned.1.call-update) | async-done | bytes 5505040 | tf_op jit(solution)/shard_map/all_gather | solution.py:362
  97.7 4.0 %first_matmul.1 = bf16[8,2,16,1536]{3,2,1,0:T(8,128)(2,1)} custom-call(bf16[2,2,128,896]{3,2,1,0:T(8,128)(2,1)S(1)} %reshape.126.rows, bf16[16,1344,128]{2,1,0:T(8,128)(2,1)} %bitcast.55), custom_call_target="tpu_custom_call" | custom-call | tf_op jit(solution)/shard_map/first_matmul/pallas_call | solution.py:150
  101.7 5.0 %all-to-all-start.2 = ((bf16[8,2,16,1536]{3,2,1,0:T(8,128)(2,1)}), bf16[8,2,16,1536]{3,2,1,0:T(8,128)(2,1)S(1)}, u32[]{:S(2)}, u32[]{:S(2)}) async-start(bf16[8,2,16,1536]{3,2,1,0:T(8,128)(2,1)} %first_matmul.1), calls=%async_computation.2 | async-start | bytes 1572864 | tf_op jit(solution)/shard_map/all_to_all | solution.py:345
  106.8 8.3 %all-to-all-done.2.parts = bf16[8,2,16,1536]{3,2,1,0:T(8,128)(2,1)S(1)} async-done(((bf16[8,2,16,1536]{3,2,1,0:T(8,128)(2,1)}), bf16[8,2,16,1536]{3,2,1,0:T(8,128)(2,1)S(1)}, u32[]{:S(2)}, u32[]{:S(2)}) %all-to-all-start.2) | async-done | bytes 786464 | tf_op jit(solution)/shard_map/all_to_all | solution.py:345
  115.1 1.1 activate.1
  116.3 3.5 %all-to-all-start.3 = ((bf16[8,2,16,1536]{3,2,1,0:T(8,128)(2,1)}), bf16[8,2,16,1536]{3,2,1,0:T(8,128)(2,1)S(1)}, u32[]{:S(2)}, u32[]{:S(2)}) async-start(bf16[8,2,16,1536]{3,2,1,0:T(8,128)(2,1)} %activate.1), calls=%async_computation.3 | async-start | bytes 1572864 | tf_op jit(solution)/shard_map/all_to_all | solution.py:345
  119.8 8.2 %all-to-all-done.3.hidden = bf16[8,2,16,1536]{3,2,1,0:T(8,128)(2,1)S(1)} async-done(((bf16[8,2,16,1536]{3,2,1,0:T(8,128)(2,1)}), bf16[8,2,16,1536]{3,2,1,0:T(8,128)(2,1)S(1)}, u32[]{:S(2)}, u32[]{:S(2)}) %all-to-all-start.3) | async-done | bytes 786464 | tf_op jit(solution)/shard_map/all_to_all | solution.py:345
  128.0 2.6 %second_matmul.3 = bf16[2,128,896]{2,1,0:T(8,128)(2,1)S(1)} custom-call(s32[1]{0:T(128)} %bitcast.23.half, bf16[8,2,16,1536]{3,2,1,0:T(8,128)(2,1)S(1)} %all-to-all-done.3.hidden, bf16[16,1344,128]{2,1,0:T(8,128)(2,1)} %bitcast.56), custom_call_target="tpu_custom_call" | custom-call | tf_op jit(solution)/shard_map/second_matmul/pallas_call | solution.py:238
  130.7 12.6 %collective-permute-start.2 = (bf16[2,128,896]{2,1,0:T(8,128)(2,1)S(1)}, bf16[2,128,896]{2,1,0:T(8,128)(2,1)S(1)}, u32[]{:S(2)}, u32[]{:S(2)}) collective-permute-start(bf16[2,128,896]{2,1,0:T(8,128)(2,1)S(1)} %second_matmul.3), channel_id=1, source_target_pairs={{0,64},{64,0},{1,65},{65,1},{2,66},{66,2},{3,67},{67,3},{4,68},{68... | collective-permute-start | bytes 1376264 | tf_op jit(solution)/shard_map/ppermute | solution.py:390
  143.3 2.7 %second_matmul.2.kept = f32[2,128,896]{2,1,0:T(8,128)S(1)} custom-call(s32[1]{0:T(128)S(6)} %sub.23.half, bf16[8,2,16,1536]{3,2,1,0:T(8,128)(2,1)S(1)} %all-to-all-done.3.hidden, bf16[16,1344,128]{2,1,0:T(8,128)(2,1)} %bitcast.57), custom_call_target="tpu_custom_call" | custom-call | tf_op jit(solution)/shard_map/second_matmul/pallas_call | solution.py:238
  146.0 1.1 merge.1
  147.1 7.1 %all-to-all-start.4 = ((bf16[64,4,896]{2,1,0:T(4,128)(2,1)}), bf16[64,4,896]{2,1,0:T(4,128)(2,1)S(1)}, u32[]{:S(2)}, u32[]{:S(2)}) async-start(bf16[64,4,896]{2,1,0:T(4,128)(2,1)} %merge.1), calls=%async_computation.4 | async-start | bytes 917504 | tf_op jit(solution)/shard_map/all_to_all | solution.py:345
  154.3 17.1 %all-to-all-done.4 = bf16[64,4,896]{2,1,0:T(4,128)(2,1)S(1)} async-done(((bf16[64,4,896]{2,1,0:T(4,128)(2,1)}), bf16[64,4,896]{2,1,0:T(4,128)(2,1)S(1)}, u32[]{:S(2)}, u32[]{:S(2)}) %all-to-all-start.4) | async-done | bytes 458784 | tf_op jit(solution)/shard_map/all_to_all | solution.py:345
  171.5 1.8 %combine.1 = bf16[64,7168]{1,0:T(8,128)(2,1)} custom-call(f32[64,32]{1,0:T(8,128)S(1)} %copy.68.weight, bf16[8,32,896]{2,1,0:T(8,128)(2,1)S(1)} %reshape.133.rows), custom_call_target="tpu_custom_call" | custom-call | tf_op jit(solution)/shard_map/combine/pallas_call | solution.py:297
  (58 shorter events, 1.6 us)
Async XLA Ops:
  6.5 24.4 %copy-start = (bf16[1,64,7168]{2,1,0:T(8,128)(2,1)S(1)}, bf16[1,64,7168]{2,1,0:T(8,128)(2,1)}, u32[]{:S(2)}) copy-start(bf16[1,64,7168]{2,1,0:T(8,128)(2,1)} %param.11) | copy-start | bytes 2752516
  6.5 2.3 %copy-start.3 = (f32[1,64,2,2,128]{4,3,2,1,0:T(2,128)S(1)}, f32[1,64,2,2,128]{4,3,2,1,0:T(2,128)}, u32[]{:S(2)}) copy-start(f32[1,64,2,2,128]{4,3,2,1,0:T(2,128)} %param.17) | copy-start | bytes 393220
  6.5 23.7 %copy-start.4 = (f32[1,64,8]{1,2,0:T(8,128)S(1)}, f32[1,64,8]{1,2,0:T(8,128)}, u32[]{:S(2)}) copy-start(f32[1,64,8]{1,2,0:T(8,128)} %param.15) | copy-start | bytes 6148
  6.5 23.8 %copy-start.6 = (s32[1,64,8]{1,2,0:T(8,128)S(1)}, s32[1,64,8]{1,2,0:T(8,128)}, u32[]{:S(2)}) copy-start(s32[1,64,8]{1,2,0:T(8,128)} %param.13) | copy-start | bytes 6148
  6.5 24.0 %copy-start.5 = (f32[1,64,8]{1,2,0:T(8,128)S(1)}, f32[1,64,8]{1,2,0:T(8,128)}, u32[]{:S(2)}) copy-start(f32[1,64,8]{1,2,0:T(8,128)} %param.16) | copy-start | bytes 6148
  6.5 24.1 %copy-start.7 = (s32[1,64,8]{1,2,0:T(8,128)S(1)}, s32[1,64,8]{1,2,0:T(8,128)}, u32[]{:S(2)}) copy-start(s32[1,64,8]{1,2,0:T(8,128)} %param.14) | copy-start | bytes 6148
  6.6 91.1 %all-gather.2.cloned.1.call-start = ((), (), s32[]{:S(2)}) async-start(), calls=%async_computation.5 | async-start | bytes 5849088 | tf_op jit(solution)/shard_map/all_gather | solution.py:362
  8.8 22.4 %copy-start.2 = (bf16[1,64,7168]{2,1,0:T(8,128)(2,1)S(1)}, bf16[1,64,7168]{2,1,0:T(8,128)(2,1)}, u32[]{:S(2)}) copy-start(bf16[1,64,7168]{2,1,0:T(8,128)(2,1)} %param.12) | copy-start | bytes 2752516
  9.8 34.2 %all-to-all-start.1 = ((bf16[32,8,128]{2,1,0:T(8,128)(2,1)}), bf16[32,8,128]{2,1,0:T(8,128)(2,1)S(1)}, u32[]{:S(2)}, u32[]{:S(2)}) async-start(bf16[32,8,128]{2,1,0:T(8,128)(2,1)} %reshape.127), calls=%async_computation.1 | async-start | bytes 131072 | tf_op jit(solution)/shard_map/all_to_all | solution.py:345
  44.1 36.8 %all-to-all-start = ((bf16[64,8,896]{2,1,0:T(8,128)(2,1)}), bf16[64,8,896]{2,1,0:T(8,128)(2,1)S(1)}, u32[]{:S(2)}, u32[]{:S(2)}) async-start(bf16[64,8,896]{2,1,0:T(8,128)(2,1)} %reshape.124), calls=%async_computation | async-start | bytes 1835008 | tf_op jit(solution)/shard_map/all_to_all | solution.py:345
  54.6 5.5 %collective-permute-start = (f32[64,16]{0,1:T(8,128)S(1)}, f32[64,16]{0,1:T(8,128)S(1)}, u32[]{:S(2)}, u32[]{:S(2)}) collective-permute-start(f32[64,16]{0,1:T(8,128)S(1)} %get-tuple-element.17), channel_id=1, source_target_pairs={{0,64},{64,128},{128,192},{192,256},{256,320},{320,384},{384,448},... | collective-permute-start | bytes 12296 | tf_op jit(solution)/shard_map/ppermute | solution.py:341
  58.1 5.4 %collective-permute-start.1 = (f32[64,16]{0,1:T(8,128)S(1)}, f32[64,16]{0,1:T(8,128)S(1)}, u32[]{:S(2)}, u32[]{:S(2)}) collective-permute-start(f32[64,16]{0,1:T(8,128)S(1)} %get-tuple-element.18), channel_id=1, source_target_pairs={{0,960},{64,0},{128,64},{192,128},{256,192},{320,256},{384,320},{4... | collective-permute-start | bytes 12296 | tf_op jit(solution)/shard_map/ppermute | solution.py:341
  101.7 13.4 %all-to-all-start.2 = ((bf16[8,2,16,1536]{3,2,1,0:T(8,128)(2,1)}), bf16[8,2,16,1536]{3,2,1,0:T(8,128)(2,1)S(1)}, u32[]{:S(2)}, u32[]{:S(2)}) async-start(bf16[8,2,16,1536]{3,2,1,0:T(8,128)(2,1)} %first_matmul.1), calls=%async_computation.2 | async-start | bytes 1572864 | tf_op jit(solution)/shard_map/all_to_all | solution.py:345
  116.3 11.8 %all-to-all-start.3 = ((bf16[8,2,16,1536]{3,2,1,0:T(8,128)(2,1)}), bf16[8,2,16,1536]{3,2,1,0:T(8,128)(2,1)S(1)}, u32[]{:S(2)}, u32[]{:S(2)}) async-start(bf16[8,2,16,1536]{3,2,1,0:T(8,128)(2,1)} %activate.1), calls=%async_computation.3 | async-start | bytes 1572864 | tf_op jit(solution)/shard_map/all_to_all | solution.py:345
  130.7 15.3 %collective-permute-start.2 = (bf16[2,128,896]{2,1,0:T(8,128)(2,1)S(1)}, bf16[2,128,896]{2,1,0:T(8,128)(2,1)S(1)}, u32[]{:S(2)}, u32[]{:S(2)}) collective-permute-start(bf16[2,128,896]{2,1,0:T(8,128)(2,1)S(1)} %second_matmul.3), channel_id=1, source_target_pairs={{0,64},{64,0},{1,65},{65,1},{2,66},{66,2},{3,67},{67,3},{4,68},{68... | collective-permute-start | bytes 1376264 | tf_op jit(solution)/shard_map/ppermute | solution.py:390
  143.3 2.7 %copy-start.1 = (bf16[256,256]{1,0:T(8,128)(2,1)S(1)}, bf16[256,256]{1,0:T(8,128)(2,1)}, u32[]{:S(2)}) copy-start(bf16[256,256]{1,0:T(8,128)(2,1)} %constant.24.clone.order) | copy-start | bytes 393220
  147.1 24.3 %all-to-all-start.4 = ((bf16[64,4,896]{2,1,0:T(4,128)(2,1)}), bf16[64,4,896]{2,1,0:T(4,128)(2,1)S(1)}, u32[]{:S(2)}, u32[]{:S(2)}) async-start(bf16[64,4,896]{2,1,0:T(4,128)(2,1)} %merge.1), calls=%async_computation.4 | async-start | bytes 917504 | tf_op jit(solution)/shard_map/all_to_all | solution.py:345
Sparse Core Ops, SparseCore 0:
  10.0 87.6 all-gather.1

commit v5 on v4

--- a/solution.py
+++ b/solution.py
@@ -20,6 +20,8 @@
 NAMES = PP + EP
 INTERPRET = False
 GROUP = 4
+PAIR = 2
+AHEAD = 2
 
 BF = jnp.bfloat16
 F32 = jnp.float32
@@ -126,11 +128,13 @@
         )
         for i in range(total // GROUP)
     ]
-    for copy in copies:
+    for copy in copies[:AHEAD]:
         copy.start()
     for i, copy in enumerate(copies):
         h, j = divmod(i, total // GROUP // halves)
         copy.wait()
+        if i + AHEAD < len(copies):
+            copies[i + AHEAD].start()
         pre = dot_nn(rows[0, h], up_columns(weights, GROUP * i, GROUP, width)).astype(BF)
         grad = dot_nt(rows[1, h], down_rows(weights, GROUP * i, GROUP, width)).astype(BF)
         for chip in range(chips):
@@ -208,24 +212,26 @@
     slices = weights.shape[0]
     copies = [
         pltpu.make_async_copy(
-            source.at[pl.ds(slices * h + GROUP * j, GROUP)],
-            weights.at[GROUP * j : GROUP * (j + 1)],
+            source.at[pl.ds(slices * h + PAIR * j, PAIR)],
+            weights.at[PAIR * j : PAIR * (j + 1)],
             sems.at[j],
         )
-        for j in range(slices // GROUP)
+        for j in range(slices // PAIR)
     ]
-    for copy in copies:
+    for copy in copies[:AHEAD]:
         copy.start()
     rows = jnp.concatenate([hidden[chip, h] for chip in range(hidden.shape[0])], axis=0)
     fwd = None
     bwd = None
     for j, copy in enumerate(copies):
         copy.wait()
-        ats = [3 * LANES * (j * GROUP // 2 + k) for k in range(GROUP // 2)]
+        if j + AHEAD < len(copies):
+            copies[j + AHEAD].start()
+        ats = [3 * LANES * (j * PAIR // 2 + k) for k in range(PAIR // 2)]
         hid = jnp.concatenate([rows[:, at + 2 * LANES : at + 3 * LANES] for at in ats], axis=1)
         grads = jnp.concatenate([rows[:, at : at + 2 * LANES] for at in ats], axis=1)
-        more_f = dot_nn(hid, down_rows(weights, GROUP * j, GROUP, width))
-        more_b = dot_nt(grads, up_columns(weights, GROUP * j, GROUP, width))
+        more_f = dot_nn(hid, down_rows(weights, PAIR * j, PAIR, width))
+        more_b = dot_nt(grads, up_columns(weights, PAIR * j, PAIR, width))
         fwd = more_f if fwd is None else fwd + more_f
         bwd = more_b if bwd is None else bwd + more_b
     out[0] = fwd.astype(out.dtype)
@@ -246,7 +252,7 @@
         out_shape=jax.ShapeDtypeStruct((2, chips * per_chip, width), dtype),
         scratch_shapes=[
             pltpu.VMEM((slices,) + weights.shape[1:], BF),
-            pltpu.SemaphoreType.DMA((slices // GROUP,)),
+            pltpu.SemaphoreType.DMA((slices // PAIR,)),
         ],
         interpret=INTERPRET,
         compiler_params=SMALL,

time: 181 us -> 182 us (level)
  transfers between devices with their start and end apart: 9 -> 9, of which waited for: 7 -> 7; matrix products, arithmetic and copies ran while one was open for 4% -> 4% of each run, Pallas kernels for 1% -> 2%
where the time goes in v5:
time: 182 us; the launch traced here: 181 us
  waiting for transfers between devices  79.9 us (44%)
  starting transfers between devices  64.3 us (35%)
  Pallas kernels  16.7 us (9%)
  between operations  13.8 us (8%)
  local copies, waits for them, and re-layouts  5.53 us (3%)
    all_to_all x5, waiting for transfers between devices, all_to_all(): return lax.all_to_all(value, axes, split_axis=0, concat_axis=0, tiled=True)  61.1 us
    all_to_all x5, starting transfers between devices, all_to_all(): return lax.all_to_all(value, axes, split_axis=0, concat_axis=0, tiled=True)  46.3 us
    all_gather x1, waiting for transfers between devices, body(): weights = lax.all_gather(packed, Z, axis=0, tiled=True)  15.3 us
    ppermute x1, starting transfers between devices, body(): other = lax.ppermute(sent, 'core', [(0, 1), (1, 0)])  12.5 us
    pallas_call x2, Pallas kernels, second_matmul(): pl.pallas_call(second_matmul_kernel, in_specs=[pl.BlockSpec(memory_space=...  5.84 us
    ppermute x2, starting transfers between devices, shifted(): return lax.ppermute(value, PP, pairs)  5.45 us
    pallas_call x1, Pallas kernels, first_matmul(): pl.pallas_call(first_matmul_kernel, in_specs=[VMEM_SPEC, pl.BlockSpec(mem...  4.62 us
  transfers between devices with their start and end apart: 9, of which 7 were waited for; matrix products, arithmetic and copies ran while one was open for 4% of the time, Pallas kernels for 2%

profile of v5, /device:TPU:1, one launch (start us, length us, event | category | flops | bytes accessed | tf_op | source)
XLA Modules:
  0.0 181.2 jit_solution(6016151391713531915)
XLA Ops:
  6.6 2.2 %pack_weights.1 = bf16[1344,128]{1,0:T(8,128)(2,1)} custom-call(bf16[7168,128]{1,0:T(8,128)(2,1)} %gate.1, bf16[7168,128]{1,0:T(8,128)(2,1)} %up.1, bf16[128,7168]{1,0:T(8,128)(2,1)} %down.1), custom_call_target="tpu_custom_call" | custom-call | tf_op jit(solution)/shard_map/pack_weights/pallas_call | solution.py:90
  9.1 0.7 reshape.127
  9.8 20.4 %all-to-all-start.1 = ((bf16[32,8,128]{2,1,0:T(8,128)(2,1)}), bf16[32,8,128]{2,1,0:T(8,128)(2,1)S(1)}, u32[]{:S(2)}, u32[]{:S(2)}) async-start(bf16[32,8,128]{2,1,0:T(8,128)(2,1)} %reshape.127), calls=%async_computation.1 | async-start | bytes 131072 | tf_op jit(solution)/shard_map/all_to_all | solution.py:351
  30.9 0.2 convolution_convert_fusion.1
  31.2 0.2 convolution_convert_fusion
  31.6 0.5 copy.62
  32.1 0.5 broadcast_in_dim.4
  32.5 1.3 reshape.124
  33.8 10.3 %all-to-all-done.1 = bf16[32,8,128]{2,1,0:T(8,128)(2,1)S(1)} async-done(((bf16[32,8,128]{2,1,0:T(8,128)(2,1)}), bf16[32,8,128]{2,1,0:T(8,128)(2,1)S(1)}, u32[]{:S(2)}, u32[]{:S(2)}) %all-to-all-start.1) | async-done | bytes 65568 | tf_op jit(solution)/shard_map/all_to_all | solution.py:351
  44.1 10.2 %all-to-all-start = ((bf16[64,8,896]{2,1,0:T(8,128)(2,1)}), bf16[64,8,896]{2,1,0:T(8,128)(2,1)S(1)}, u32[]{:S(2)}, u32[]{:S(2)}) async-start(bf16[64,8,896]{2,1,0:T(8,128)(2,1)} %reshape.124), calls=%async_computation | async-start | bytes 1835008 | tf_op jit(solution)/shard_map/all_to_all | solution.py:351
  54.6 3.5 %collective-permute-start = (f32[64,16]{0,1:T(8,128)S(1)}, f32[64,16]{0,1:T(8,128)S(1)}, u32[]{:S(2)}, u32[]{:S(2)}) collective-permute-start(f32[64,16]{0,1:T(8,128)S(1)} %get-tuple-element.17), channel_id=1, source_target_pairs={{0,64},{64,128},{128,192},{192,256},{256,320},{320,384},{384,448},... | collective-permute-start | bytes 12296 | tf_op jit(solution)/shard_map/ppermute | solution.py:347
  58.1 1.9 %collective-permute-start.1 = (f32[64,16]{0,1:T(8,128)S(1)}, f32[64,16]{0,1:T(8,128)S(1)}, u32[]{:S(2)}, u32[]{:S(2)}) collective-permute-start(f32[64,16]{0,1:T(8,128)S(1)} %get-tuple-element.18), channel_id=1, source_target_pairs={{0,960},{64,0},{128,64},{192,128},{256,192},{320,256},{384,320},{4... | collective-permute-start | bytes 12296 | tf_op jit(solution)/shard_map/ppermute | solution.py:347
  60.0 3.4 %collective-permute-done.1 = f32[64,16]{0,1:T(8,128)S(1)} collective-permute-done((f32[64,16]{0,1:T(8,128)S(1)}, f32[64,16]{0,1:T(8,128)S(1)}, u32[]{:S(2)}, u32[]{:S(2)}) %collective-permute-start.1) | collective-permute-done | bytes 4128 | tf_op jit(solution)/shard_map/ppermute | solution.py:347
  63.7 0.1 reshape.129
  63.8 17.1 %all-to-all-done = bf16[64,8,896]{2,1,0:T(8,128)(2,1)S(1)} async-done(((bf16[64,8,896]{2,1,0:T(8,128)(2,1)}), bf16[64,8,896]{2,1,0:T(8,128)(2,1)S(1)}, u32[]{:S(2)}, u32[]{:S(2)}) %all-to-all-start) | async-done | bytes 917536 | tf_op jit(solution)/shard_map/all_to_all | solution.py:351
  80.9 0.1 copy.63
  81.1 0.9 copy.64
  82.0 0.3 reshape.126.rows
  82.4 15.3 %all-gather.2.cloned.1.call-done = bf16[21504,128]{1,0:T(8,128)(2,1)} async-done(((bf16[1344,128]{1,0:T(8,128)(2,1)}), bf16[21504,128]{1,0:T(8,128)(2,1)}) %all-gather.2.cloned.1.call-update) | async-done | bytes 5505040 | tf_op jit(solution)/shard_map/all_gather | solution.py:368
  97.7 4.6 %first_matmul.1 = bf16[8,2,16,1536]{3,2,1,0:T(8,128)(2,1)} custom-call(bf16[2,2,128,896]{3,2,1,0:T(8,128)(2,1)S(1)} %reshape.126.rows, bf16[16,1344,128]{2,1,0:T(8,128)(2,1)} %bitcast.55), custom_call_target="tpu_custom_call" | custom-call | tf_op jit(solution)/shard_map/first_matmul/pallas_call | solution.py:154
  102.3 5.0 %all-to-all-start.2 = ((bf16[8,2,16,1536]{3,2,1,0:T(8,128)(2,1)}), bf16[8,2,16,1536]{3,2,1,0:T(8,128)(2,1)S(1)}, u32[]{:S(2)}, u32[]{:S(2)}) async-start(bf16[8,2,16,1536]{3,2,1,0:T(8,128)(2,1)} %first_matmul.1), calls=%async_computation.2 | async-start | bytes 1572864 | tf_op jit(solution)/shard_map/all_to_all | solution.py:351
  107.4 8.3 %all-to-all-done.2.parts = bf16[8,2,16,1536]{3,2,1,0:T(8,128)(2,1)S(1)} async-done(((bf16[8,2,16,1536]{3,2,1,0:T(8,128)(2,1)}), bf16[8,2,16,1536]{3,2,1,0:T(8,128)(2,1)S(1)}, u32[]{:S(2)}, u32[]{:S(2)}) %all-to-all-start.2) | async-done | bytes 786464 | tf_op jit(solution)/shard_map/all_to_all | solution.py:351
  115.7 1.1 activate.1
  116.8 3.5 %all-to-all-start.3 = ((bf16[8,2,16,1536]{3,2,1,0:T(8,128)(2,1)}), bf16[8,2,16,1536]{3,2,1,0:T(8,128)(2,1)S(1)}, u32[]{:S(2)}, u32[]{:S(2)}) async-start(bf16[8,2,16,1536]{3,2,1,0:T(8,128)(2,1)} %activate.1), calls=%async_computation.3 | async-start | bytes 1572864 | tf_op jit(solution)/shard_map/all_to_all | solution.py:351
  120.4 8.2 %all-to-all-done.3.hidden = bf16[8,2,16,1536]{3,2,1,0:T(8,128)(2,1)S(1)} async-done(((bf16[8,2,16,1536]{3,2,1,0:T(8,128)(2,1)}), bf16[8,2,16,1536]{3,2,1,0:T(8,128)(2,1)S(1)}, u32[]{:S(2)}, u32[]{:S(2)}) %all-to-all-start.3) | async-done | bytes 786464 | tf_op jit(solution)/shard_map/all_to_all | solution.py:351
  128.6 2.9 %second_matmul.3 = bf16[2,128,896]{2,1,0:T(8,128)(2,1)S(1)} custom-call(s32[1]{0:T(128)} %bitcast.23.half, bf16[8,2,16,1536]{3,2,1,0:T(8,128)(2,1)S(1)} %all-to-all-done.3.hidden, bf16[16,1344,128]{2,1,0:T(8,128)(2,1)} %bitcast.56), custom_call_target="tpu_custom_call" | custom-call | tf_op jit(solution)/shard_map/second_matmul/pallas_call | solution.py:244
  131.5 12.5 %collective-permute-start.2 = (bf16[2,128,896]{2,1,0:T(8,128)(2,1)S(1)}, bf16[2,128,896]{2,1,0:T(8,128)(2,1)S(1)}, u32[]{:S(2)}, u32[]{:S(2)}) collective-permute-start(bf16[2,128,896]{2,1,0:T(8,128)(2,1)S(1)} %second_matmul.3), channel_id=1, source_target_pairs={{0,64},{64,0},{1,65},{65,1},{2,66},{66,2},{3,67},{67,3},{4,68},{68... | collective-permute-start | bytes 1376264 | tf_op jit(solution)/shard_map/ppermute | solution.py:396
  144.1 2.9 %second_matmul.2.kept = f32[2,128,896]{2,1,0:T(8,128)S(1)} custom-call(s32[1]{0:T(128)S(6)} %sub.23.half, bf16[8,2,16,1536]{3,2,1,0:T(8,128)(2,1)S(1)} %all-to-all-done.3.hidden, bf16[16,1344,128]{2,1,0:T(8,128)(2,1)} %bitcast.57), custom_call_target="tpu_custom_call" | custom-call | tf_op jit(solution)/shard_map/second_matmul/pallas_call | solution.py:244
  147.1 1.1 merge.1
  148.2 7.1 %all-to-all-start.4 = ((bf16[64,4,896]{2,1,0:T(4,128)(2,1)}), bf16[64,4,896]{2,1,0:T(4,128)(2,1)S(1)}, u32[]{:S(2)}, u32[]{:S(2)}) async-start(bf16[64,4,896]{2,1,0:T(4,128)(2,1)} %merge.1), calls=%async_computation.4 | async-start | bytes 917504 | tf_op jit(solution)/shard_map/all_to_all | solution.py:351
  155.3 17.1 %all-to-all-done.4 = bf16[64,4,896]{2,1,0:T(4,128)(2,1)S(1)} async-done(((bf16[64,4,896]{2,1,0:T(4,128)(2,1)}), bf16[64,4,896]{2,1,0:T(4,128)(2,1)S(1)}, u32[]{:S(2)}, u32[]{:S(2)}) %all-to-all-start.4) | async-done | bytes 458784 | tf_op jit(solution)/shard_map/all_to_all | solution.py:351
  172.6 1.8 combine.1
  (58 shorter events, 1.6 us)
Async XLA Ops:
  6.5 24.4 %copy-start = (bf16[1,64,7168]{2,1,0:T(8,128)(2,1)S(1)}, bf16[1,64,7168]{2,1,0:T(8,128)(2,1)}, u32[]{:S(2)}) copy-start(bf16[1,64,7168]{2,1,0:T(8,128)(2,1)} %param.11) | copy-start | bytes 2752516
  6.5 2.3 %copy-start.3 = (f32[1,64,2,2,128]{4,3,2,1,0:T(2,128)S(1)}, f32[1,64,2,2,128]{4,3,2,1,0:T(2,128)}, u32[]{:S(2)}) copy-start(f32[1,64,2,2,128]{4,3,2,1,0:T(2,128)} %param.17) | copy-start | bytes 393220
  6.5 23.7 %copy-start.4 = (f32[1,64,8]{1,2,0:T(8,128)S(1)}, f32[1,64,8]{1,2,0:T(8,128)}, u32[]{:S(2)}) copy-start(f32[1,64,8]{1,2,0:T(8,128)} %param.15) | copy-start | bytes 6148
  6.5 23.8 %copy-start.6 = (s32[1,64,8]{1,2,0:T(8,128)S(1)}, s32[1,64,8]{1,2,0:T(8,128)}, u32[]{:S(2)}) copy-start(s32[1,64,8]{1,2,0:T(8,128)} %param.13) | copy-start | bytes 6148
  6.5 24.0 %copy-start.5 = (f32[1,64,8]{1,2,0:T(8,128)S(1)}, f32[1,64,8]{1,2,0:T(8,128)}, u32[]{:S(2)}) copy-start(f32[1,64,8]{1,2,0:T(8,128)} %param.16) | copy-start | bytes 6148
  6.5 24.1 %copy-start.7 = (s32[1,64,8]{1,2,0:T(8,128)S(1)}, s32[1,64,8]{1,2,0:T(8,128)}, u32[]{:S(2)}) copy-start(s32[1,64,8]{1,2,0:T(8,128)} %param.14) | copy-start | bytes 6148
  6.6 91.1 %all-gather.2.cloned.1.call-start = ((), (), s32[]{:S(2)}) async-start(), calls=%async_computation.5 | async-start | bytes 5849088 | tf_op jit(solution)/shard_map/all_gather | solution.py:368
  8.8 22.4 %copy-start.2 = (bf16[1,64,7168]{2,1,0:T(8,128)(2,1)S(1)}, bf16[1,64,7168]{2,1,0:T(8,128)(2,1)}, u32[]{:S(2)}) copy-start(bf16[1,64,7168]{2,1,0:T(8,128)(2,1)} %param.12) | copy-start | bytes 2752516
  9.8 34.2 %all-to-all-start.1 = ((bf16[32,8,128]{2,1,0:T(8,128)(2,1)}), bf16[32,8,128]{2,1,0:T(8,128)(2,1)S(1)}, u32[]{:S(2)}, u32[]{:S(2)}) async-start(bf16[32,8,128]{2,1,0:T(8,128)(2,1)} %reshape.127), calls=%async_computation.1 | async-start | bytes 131072 | tf_op jit(solution)/shard_map/all_to_all | solution.py:351
  44.1 36.8 %all-to-all-start = ((bf16[64,8,896]{2,1,0:T(8,128)(2,1)}), bf16[64,8,896]{2,1,0:T(8,128)(2,1)S(1)}, u32[]{:S(2)}, u32[]{:S(2)}) async-start(bf16[64,8,896]{2,1,0:T(8,128)(2,1)} %reshape.124), calls=%async_computation | async-start | bytes 1835008 | tf_op jit(solution)/shard_map/all_to_all | solution.py:351
  54.6 5.5 %collective-permute-start = (f32[64,16]{0,1:T(8,128)S(1)}, f32[64,16]{0,1:T(8,128)S(1)}, u32[]{:S(2)}, u32[]{:S(2)}) collective-permute-start(f32[64,16]{0,1:T(8,128)S(1)} %get-tuple-element.17), channel_id=1, source_target_pairs={{0,64},{64,128},{128,192},{192,256},{256,320},{320,384},{384,448},... | collective-permute-start | bytes 12296 | tf_op jit(solution)/shard_map/ppermute | solution.py:347
  58.1 5.4 %collective-permute-start.1 = (f32[64,16]{0,1:T(8,128)S(1)}, f32[64,16]{0,1:T(8,128)S(1)}, u32[]{:S(2)}, u32[]{:S(2)}) collective-permute-start(f32[64,16]{0,1:T(8,128)S(1)} %get-tuple-element.18), channel_id=1, source_target_pairs={{0,960},{64,0},{128,64},{192,128},{256,192},{320,256},{384,320},{4... | collective-permute-start | bytes 12296 | tf_op jit(solution)/shard_map/ppermute | solution.py:347
  102.3 13.4 %all-to-all-start.2 = ((bf16[8,2,16,1536]{3,2,1,0:T(8,128)(2,1)}), bf16[8,2,16,1536]{3,2,1,0:T(8,128)(2,1)S(1)}, u32[]{:S(2)}, u32[]{:S(2)}) async-start(bf16[8,2,16,1536]{3,2,1,0:T(8,128)(2,1)} %first_matmul.1), calls=%async_computation.2 | async-start | bytes 1572864 | tf_op jit(solution)/shard_map/all_to_all | solution.py:351
  116.8 11.8 %all-to-all-start.3 = ((bf16[8,2,16,1536]{3,2,1,0:T(8,128)(2,1)}), bf16[8,2,16,1536]{3,2,1,0:T(8,128)(2,1)S(1)}, u32[]{:S(2)}, u32[]{:S(2)}) async-start(bf16[8,2,16,1536]{3,2,1,0:T(8,128)(2,1)} %activate.1), calls=%async_computation.3 | async-start | bytes 1572864 | tf_op jit(solution)/shard_map/all_to_all | solution.py:351
  131.5 15.5 %collective-permute-start.2 = (bf16[2,128,896]{2,1,0:T(8,128)(2,1)S(1)}, bf16[2,128,896]{2,1,0:T(8,128)(2,1)S(1)}, u32[]{:S(2)}, u32[]{:S(2)}) collective-permute-start(bf16[2,128,896]{2,1,0:T(8,128)(2,1)S(1)} %second_matmul.3), channel_id=1, source_target_pairs={{0,64},{64,0},{1,65},{65,1},{2,66},{66,2},{3,67},{67,3},{4,68},{68... | collective-permute-start | bytes 1376264 | tf_op jit(solution)/shard_map/ppermute | solution.py:396
  144.1 3.0 %copy-start.1 = (bf16[256,256]{1,0:T(8,128)(2,1)S(1)}, bf16[256,256]{1,0:T(8,128)(2,1)}, u32[]{:S(2)}) copy-start(bf16[256,256]{1,0:T(8,128)(2,1)} %constant.24.clone.order) | copy-start | bytes 393220
  148.2 24.3 %all-to-all-start.4 = ((bf16[64,4,896]{2,1,0:T(4,128)(2,1)}), bf16[64,4,896]{2,1,0:T(4,128)(2,1)S(1)}, u32[]{:S(2)}, u32[]{:S(2)}) async-start(bf16[64,4,896]{2,1,0:T(4,128)(2,1)} %merge.1), calls=%async_computation.4 | async-start | bytes 917504 | tf_op jit(solution)/shard_map/all_to_all | solution.py:351
Sparse Core Ops, SparseCore 0:
  10.0 87.6 all-gather.1
